TPU v7x, 512 devices: a whole 4x4x16 slice. The times are simulated.
512 devices in a mesh: station: 32 (over x, y, core), section: 16 (over z).
Axes of the slice: x: 4, y: 4, z: 16, core: 2. Of those that a mesh axis runs over, the one named last changes fastest.
Arguments:
- voltages: bfloat16 [32, 512, 17408], P('station', 'section'), may hold values from -6 to 6
- taper: float32 [14, 1024], replicated, may hold values from -1.6 to 1.6
- beam_weight_table: bfloat16 [32, 8, 512, 2, 512], P('station', None, 'section'), may hold values from -0.5 to 0.5
- starts: int32 [8], replicated, may hold values from 0 to 15
- owner_map: int32 [512], replicated, may hold values from 0 to 31, as said below
Outputs:
- visibilities: bfloat16 [16, 32, 1, 8, 4, 64, 128], P('section', 'station')
Inputs may be any that keep to these rules, and one draw needn't show every extreme that they name: `owner_map`: within each block of 32 consecutive channels every owner 0 to 31 owns exactly 1 channels.
All inputs are finite; a program needn't handle non-finite values.
Results may differ from a plain program's by a relative error of at most 0.014.
Values may be sent and summed in bfloat16 or wider, within the bound.
No kernel may reach another device: no remote copies, remote signals or barrier semaphores. Data moves between devices by JAX's collectives and lax.ppermute only.
A program may use at most 64 MiB of HBM per device.

v0:
```python
import math

import jax
import jax.numpy as jnp
from jax import lax
from jax.sharding import PartitionSpec as P


def prefix(value, axis, join, neutral):
    count, mine = (lax.axis_size(axis), lax.axis_index(axis))
    pieces = lax.all_gather(value, axis)
    subtotal = jnp.full_like(value, 0) + jnp.asarray(neutral, value.dtype)

    def turn(position, subtotal):
        longer = join(subtotal, pieces[position])
        return jnp.where(position < mine, longer, subtotal)

    return lax.fori_loop(0, count - 1, turn, subtotal)


def spread(block, axis, source):
    block = jnp.where(lax.axis_index(axis) == source, block, jnp.zeros_like(block))
    return lax.psum(block, axis)


def dft_table(length):
    half = length // 2
    index_n = jnp.arange(length, dtype=jnp.int32)[:, None]
    index_k = jnp.arange(half, dtype=jnp.int32)[None, :]
    phase = (index_n * index_k % length).astype(jnp.float32) * (2.0 * math.pi / length)
    factor = 1.0 / math.sqrt(length)
    return jnp.concatenate([jnp.cos(phase) * factor, -jnp.sin(phase) * factor], axis=1).astype(
        jnp.bfloat16
    )


def add_terms(earlier, later):
    return earlier + later


def local(voltages, taper, beam_weight_table, starts, owner_map):
    inputs = voltages.shape[1]
    length = taper.shape[1]
    tap_count = taper.shape[0]
    frames = voltages.shape[2] // length - tap_count + 1
    channels = length // 2
    beam_count = beam_weight_table.shape[1]
    antennas = inputs // 2
    sections = lax.axis_size("section")
    stations = lax.axis_size("station")
    section = lax.axis_index("section")
    span_count = max(1, sections // 2)
    block = channels // sections
    per_owner = block // stations
    framed = voltages[0].reshape(inputs, frames + tap_count - 1, length)
    filtered = jnp.zeros((inputs, frames, length), jnp.float32)
    for tap in range(tap_count):
        filtered = filtered + taper[tap][None, None, :] * framed[:, tap : tap + frames, :].astype(
            jnp.float32
        )
    rows = filtered.astype(jnp.bfloat16).reshape(inputs * frames, length)
    spectra = jnp.dot(rows, dft_table(length), preferred_element_type=jnp.float32)
    spectra = spectra.reshape(antennas, 2, frames, 2, channels)
    real_x = spectra[:, :, :, 0, :]
    imag_x = spectra[:, :, :, 1, :]
    offset = jnp.remainder(section - starts, sections)
    inside = (offset < span_count).astype(jnp.float32)
    scaled = beam_weight_table[0].astype(jnp.float32).reshape(beam_count, antennas, 2, 2, channels)
    scaled = scaled * inside[:, None, None, None, None]
    real_w = scaled[:, :, :, 0, :]
    imag_w = scaled[:, :, :, 1, :]
    real_b = jnp.einsum("bapk,apfk->kbpf", real_w, real_x) - jnp.einsum(
        "bapk,apfk->kbpf", imag_w, imag_x
    )
    imag_b = jnp.einsum("bapk,apfk->kbpf", real_w, imag_x) + jnp.einsum(
        "bapk,apfk->kbpf", imag_w, real_x
    )
    partial_sum = jnp.stack([real_b, imag_b], axis=3).reshape(channels, beam_count * 4 * frames)
    earlier_sum = prefix(partial_sum, "section", add_terms, jnp.zeros_like(partial_sum))
    complete = (earlier_sum + partial_sum).astype(jnp.bfloat16)
    complete = spread(complete, "section", sections - 1)
    mine = lax.dynamic_slice_in_dim(complete, section * block, block, 0)
    owners_here = lax.dynamic_slice_in_dim(owner_map, section * block, block, 0)
    ranked = jnp.argsort(owners_here, stable=True)
    placed = jnp.take(mine, ranked, axis=0)
    arrived = lax.all_to_all(placed, "station", split_axis=0, concat_axis=0, tiled=True)
    gathered = arrived.reshape(stations, per_owner, beam_count, 2, 2, frames)
    gathered = jnp.transpose(gathered, (1, 2, 5, 0, 3, 4)).astype(jnp.float32)
    real_z = gathered[..., 0].reshape(per_owner, beam_count, frames, 2 * stations)
    imag_z = gathered[..., 1].reshape(per_owner, beam_count, frames, 2 * stations)
    real_v = jnp.einsum("cbfi,cbfj->cbfij", real_z, real_z) + jnp.einsum(
        "cbfi,cbfj->cbfij", imag_z, imag_z
    )
    imag_v = jnp.einsum("cbfi,cbfj->cbfij", imag_z, real_z) - jnp.einsum(
        "cbfi,cbfj->cbfij", real_z, imag_z
    )
    visible = jnp.concatenate([real_v, imag_v], axis=-1).astype(jnp.bfloat16)
    return visible.reshape(1, 1, per_owner, beam_count, frames, 2 * stations, 4 * stations)


def solution(mesh):
    placed = (
        P("station", "section", None),
        P(),
        P("station", None, "section", None, None),
        P(),
        P(),
    )
    return jax.shard_map(
        local,
        mesh=mesh,
        in_specs=placed,
        out_specs=P("section", "station", None, None, None, None, None),
        check_vma=False,
    )
```

profile of v0, /device:TPU:1, one launch (start us, length us, event | category | flops | bytes accessed | tf_op | source)
XLA Modules:
  0.0 303.3 jit_solution(7229301589758083109)
XLA Ops:
  6.5 9.2 %multiply_convert_fusion = (bf16[1024,512]{0,1:T(8,128)(2,1)S(1)}, bf16[1024,512]{0,1:T(8,128)(2,1)}) fusion(), kind=kLoop, calls=%fused_computation.19 | loop fusion | flops 9961472 | bytes 2097152 | tf_op jit(solution)/shard_map/convert.18
  15.8 1.7 reshape_squeeze.2
  17.5 1.4 pad_maximum_fusion.1
  18.9 2.0 add_convert_fusion.1
  22.9 5.3 %copy.70 = f32[8,16,2,2,512]{1,0,2,4,3:T(8,128)} copy(bf16[8,16,2,2,512]{4,0,3,2,1:T(8,128)(2,1)S(1)} %bitcast.75) | data formatting | bytes 1572864 | tf_op jit(solution)/shard_map/convert_element_type | solution.py:68
  28.9 4.1 %broadcast_multiply_fusion = bf16[8,16,2,2,512]{1,0,2,4,3:T(8,128)(2,1)S(1)} fusion(f32[8,16,2,2,512]{1,0,2,4,3:T(8,128)} %copy.70, f32[8]{0:T(128)S(1)} %compare_convert_fusion), kind=kLoop, calls=%fused_computation.5 | loop fusion | flops 524288 | bytes 1572896 | tf_op jit(solution)/shard_map/mul | solution.py:69
  33.0 1.3 fusion.1
  34.3 1.3 fusion
  35.6 1.3 subtract_bitcast_fusion
  36.9 1.3 add_bitcast_fusion
  38.1 3.0 pad_maximum_fusion
  41.1 3.5 %copy.75 = f32[512,8,2,2,4]{0,4,3,2,1:T(4,128)S(1)} copy(f32[512,8,2,2,4]{1,4,2,0,3:T(4,128)} %pad_maximum_fusion) | data formatting | bytes 524288 | tf_op jit(solution)/shard_map/stack | solution.py:78
  46.6 1.6 sort.17
  48.3 72.0 %all-gather.2.cloned.1.call-done = f32[16,512,128]{2,1,0:T(8,128)} async-done(((f32[1,512,128]{2,1,0:T(8,128)}), f32[16,512,128]{2,1,0:T(8,128)}) %all-gather.2.cloned.1.call-update) | async-done | bytes 4194320 | tf_op jit(solution)/shard_map/all_gather | solution.py:11
  120.3 15.7 %while.14 = (s32[]{:T(128)}, f32[512,128]{1,0:T(8,128)S(1)}, s32[]{:T(128)}, f32[16,512,128]{2,1,0:T(8,128)}, s32[]{:T(128)}, /*index=5*/s32[]{:T(128)}) while((s32[]{:T(128)}, f32[512,128]{1,0:T(8,128)S(1)}, s32[]{:T(128)}, f32[16,512,128]{2,1,0:T(8,128)}, s32[]{:T(128)}, /*index=5*/s32[]{:T(128)}) %tuple.50), condition=%wide.region_2.3_spmd.clone, body=%wide.region_1.2_spmd.clone.sunk | while | flops 196612 | bytes 786525 | solution.py:18
  121.3 1.0 add_select_fusion.3
  122.4 1.0 add_select_fusion.3
  123.4 1.0 add_select_fusion.3
  124.4 1.0 add_select_fusion.3
  125.5 1.0 add_select_fusion.3
  126.5 1.0 add_select_fusion.3
  136.7 132.5 %all-reduce.2.cloned.1.call-done = bf16[512,128]{1,0:T(8,128)(2,1)} async-done(((bf16[512,128]{1,0:T(8,128)(2,1)}), bf16[512,128]{1,0:T(8,128)(2,1)}) %all-reduce.2.cloned.1.call-update) | async-done | bytes 131088 | tf_op jit(solution)/shard_map/psum | solution.py:23
  270.6 23.5 %all_to_all.6 = bf16[32,1,128]{2,1,0:T(2,128)(2,1)S(1)} all-to-all(bf16[32,1,128]{2,1,0:T(2,128)(2,1)S(1)} %copy.79), channel_id=1, replica_groups=mesh['station'=32,'section'=16] {'station'}, dimensions={0} | all-to-all | bytes 16384 | tf_op jit(solution)/shard_map/all_to_all | solution.py:86
  295.4 1.1 pad_maximum_fusion.2
  (49 shorter events, 17.3 us)
Async XLA Ops:
  6.5 9.2 %copy-start.1 = (f32[14,1024]{1,0:T(8,128)S(1)}, f32[14,1024]{1,0:T(8,128)}, u32[]{:S(2)}) copy-start(f32[14,1024]{1,0:T(8,128)} %param.8) | copy-start | bytes 172036
  6.5 113.7 %all-gather.2.cloned.1.call-start = ((), (), s32[]{:S(2)}) async-start(), calls=%async_computation.1 | async-start | bytes 4456448 | tf_op jit(solution)/shard_map/all_gather | solution.py:11
  20.8 1.6 copy-start
  22.9 6.0 %copy-start.2 = (s32[8]{0:T(128)S(1)}, s32[8]{0:T(128)}, u32[]{:S(2)}) copy-start(s32[8]{0:T(128)} %param.10) | copy-start | bytes 100
  45.6 223.6 %all-reduce.2.cloned.1.call-start = ((), (), s32[]{:S(2)}) async-start(), calls=%async_computation.2 | async-start | bytes 262144 | tf_op jit(solution)/shard_map/psum | solution.py:23
Sparse Core Ops, SparseCore 0:
  45.7 74.5 all-gather.1
  136.8 132.3 all-reduce.1
where the time goes:
time: 304 us; the launch traced here: 303 us
  waiting for transfers between devices  205 us (67%)
  other arithmetic  39.3 us (13%)
  blocking collectives  23.5 us (8%)
  local copies, waits for them, and re-layouts  16 us (5%)
  between operations  13.6 us (4%)
  matrix products  5.93 us (2%)
    psum x1, waiting for transfers between devices, spread(): return lax.psum(block, axis)  133 us
    all_gather x1, waiting for transfers between devices, prefix(): pieces = lax.all_gather(value, axis)  72 us
    all_to_all x1, blocking collectives, local(): lax.all_to_all(placed, 'station', split_axis=0, concat_axis=0, tiled=True)  23.5 us
    select_n x15, other arithmetic, turn(): return jnp.where(position < mine, longer, subtotal)  15.4 us
    another operation x2, other arithmetic  9.23 us
  transfers between devices with their start and end apart: 2, of which 2 were waited for; matrix products, arithmetic and copies ran while one was open for 1% of the time, Pallas kernels for 0%

commit v1 on v0

v1 whole, which is shorter than its diff:
```python
import functools
import math

import jax
import jax.numpy as jnp
import ml_dtypes
import numpy as np
from jax import lax
from jax.experimental import pallas as pl
from jax.experimental.pallas import tpu as pltpu
from jax.sharding import PartitionSpec as P

LANES = 128
F32 = jnp.float32
BF16 = jnp.bfloat16


def dft_table(length):
    half = length // 2
    n = np.arange(length, dtype=np.int32)[:, None]
    k = np.arange(half, dtype=np.int32)[None, :]
    phase = (n * k % length).astype(np.float32) * np.float32(2.0 * math.pi / length)
    factor = np.float32(1.0 / math.sqrt(length))
    real = (np.cos(phase) * factor).reshape(length, half // LANES, LANES)
    imag = (-np.sin(phase) * factor).reshape(length, half // LANES, LANES)
    return np.concatenate([real, imag], axis=2).reshape(length, length).astype(ml_dtypes.bfloat16)


def front_kernel(
    dims, starts_ref, section_ref, owner_ref, taper_ref, volts_hbm, weights_hbm, table_hbm,
    out_ref, volts, weights, table, rows, beams, sems,
):
    inputs, taps, frames, length, beam_count, sections, stations = dims
    channels = length // 2
    chunks = channels // LANES
    block = channels // sections
    half = 16
    parts = inputs // half
    volt_copies = [
        pltpu.make_async_copy(
            volts_hbm.at[0, pl.ds(i * half, half)], volts.at[pl.ds(i * half, half)], sems.at[i]
        )
        for i in range(parts)
    ]
    table_copies = [
        pltpu.make_async_copy(
            table_hbm.at[:, pl.ds(c * 2 * LANES, 2 * LANES)], table.at[c], sems.at[parts + c]
        )
        for c in range(chunks)
    ]
    weight_copy = pltpu.make_async_copy(weights_hbm, weights, sems.at[parts + chunks])
    for copy in volt_copies + table_copies:
        copy.start()
    weight_copy.start()

    for i in range(parts):
        volt_copies[i].wait()
        for c in range(length // LANES):
            at = c * LANES
            taper = [
                jnp.broadcast_to(taper_ref[pl.ds(t, 1), pl.ds(at, LANES)], (half, LANES))
                for t in range(taps)
            ]
            sums = [None] * frames
            for g in range(frames + taps - 1):
                value = volts[pl.ds(i * half, half), pl.ds(g * length + at, LANES)].astype(F32)
                for f in range(frames):
                    t = g - f
                    if 0 <= t < taps:
                        term = taper[t] * value
                        sums[f] = term if sums[f] is None else sums[f] + term
            for f in range(frames):
                rows[pl.ds(f * inputs + i * half, half), pl.ds(at, LANES)] = sums[f].astype(BF16)

    section = section_ref[0]
    keep = [
        jnp.where(((section - starts_ref[b] + sections) & (sections - 1)) < sections // 2, 1.0, 0.0)
        for b in range(beam_count)
    ]
    row = lax.broadcasted_iota(jnp.int32, (8, LANES), 0)
    low = row < 4
    first = (row & 2) == 0
    tiles = inputs // 8

    def tile_of(array, start):
        return lax.slice(array, (start, 0), (start + 8, LANES))

    for c in range(chunks):
        table_copies[c].wait()
        spectra = jnp.dot(rows[...], table[c], preferred_element_type=F32)
        real_x = lax.slice(spectra, (0, 0), (frames * inputs, LANES))
        imag_x = lax.slice(spectra, (0, LANES), (frames * inputs, 2 * LANES))
        if c == 0:
            weight_copy.wait()
        for b in range(beam_count):
            real_w = weights[b, 0, :, pl.ds(c * LANES, LANES)].astype(F32)
            imag_w = weights[b, 1, :, pl.ds(c * LANES, LANES)].astype(F32)
            sums = [[], []]
            for f in range(frames):
                real = imag = None
                for i in range(tiles):
                    xr = tile_of(real_x, f * inputs + i * 8)
                    xi = tile_of(imag_x, f * inputs + i * 8)
                    wr = tile_of(real_w, i * 8)
                    wi = tile_of(imag_w, i * 8)
                    re = wr * xr - wi * xi
                    im = wr * xi + wi * xr
                    real = re if real is None else real + re
                    imag = im if imag is None else imag + im
                sums[0].append(real)
                sums[1].append(imag)
            for part in range(2):
                v = sums[part]
                pairs = []
                for one, two in ((v[0], v[1]), (v[2], v[3])):
                    pairs.append(
                        jnp.where(low, one, two) + pltpu.roll(jnp.where(low, two, one), 4, 0)
                    )
                one = pairs[0] + pltpu.roll(pairs[0], 6, 0)
                two = pairs[1] + pltpu.roll(pairs[1], 2, 0)
                beams[pl.ds(b * 16 + part * 8, 8), pl.ds(c * LANES, LANES)] = (
                    jnp.where(first, one, two) * keep[b]
                )

    per = LANES // block
    for c in range(chunks):
        owners = owner_ref[pl.ds(0, 1), pl.ds(c * LANES, LANES)]
        lane = lax.broadcasted_iota(jnp.int32, (1, LANES), 1)
        target = (lane // block) * block + owners
        slot = lax.broadcasted_iota(jnp.int32, (LANES, LANES), 0)
        pick = jnp.where(slot == target, 1.0, 0.0).astype(BF16)
        values = beams[:, pl.ds(c * LANES, LANES)].astype(BF16)
        placed = lax.dot_general(
            pick, values, (((1,), (1,)), ((), ())), preferred_element_type=F32
        ).astype(BF16)
        for s in range(per):
            out_ref[c * per + s] = lax.slice(placed, (s * block, 0), ((s + 1) * block, LANES))


def place_of(beam, frame, part, pol):
    return beam * 16 + part * 8 + (frame & 1) * 4 + (frame >> 1) * 2 + pol


def selectors(beam_count, frames, stations):
    pairs = beam_count * frames
    pick = np.zeros((4 * pairs, LANES), np.float32)
    columns = np.zeros((2, LANES, 2 * pairs), np.float32)
    for b in range(beam_count):
        for f in range(frames):
            for part in range(2):
                for pol in range(2):
                    j = place_of(b, f, part, pol)
                    pick[(part * 2 + pol) * pairs + b * frames + f, j] = 1
                    columns[pol, j, part * pairs + b * frames + f] = 1
    spread = np.zeros((2, stations, 2 * stations), np.float32)
    for st in range(stations):
        for pol in range(2):
            spread[pol, st, 2 * st + pol] = 1
    zero = np.zeros_like(spread)
    left = np.concatenate([spread, zero], axis=2)
    right = np.concatenate([zero, spread], axis=2)
    first = np.stack([left, -right])
    second = np.stack([right, left])
    rows = np.stack([first, second])
    as_type = lambda a: a.astype(ml_dtypes.bfloat16)
    return as_type(pick), as_type(columns), as_type(np.swapaxes(spread, 1, 2)), as_type(rows)


def back_kernel(dims, z_ref, pick_ref, columns_ref, spread_ref, rows_ref, out_hbm, out, sems):
    beam_count, frames, stations = dims
    pairs = beam_count * frames
    z = z_ref[...].astype(BF16)
    turned = lax.dot_general(
        pick_ref[...], z, (((1,), (1,)), ((), ())), preferred_element_type=F32
    ).astype(BF16)
    row_values = []
    for kind in range(2):
        total = None
        for part in range(2):
            for pol in range(2):
                at = (part * 2 + pol) * pairs
                term = jnp.dot(
                    lax.slice(turned, (at, 0), (at + pairs, stations)),
                    rows_ref[kind, part, pol],
                    preferred_element_type=F32,
                )
                total = term if total is None else total + term
        row_values.append(total)
    column = None
    for pol in range(2):
        chosen = jnp.dot(z, columns_ref[pol], preferred_element_type=F32).astype(BF16)
        term = jnp.dot(spread_ref[pol], chosen, preferred_element_type=F32)
        column = term if column is None else column + term
    ends = []
    for b in range(beam_count):
        for f in range(frames):
            at = b * frames + f
            real = jnp.broadcast_to(
                lax.slice(column, (0, at), (2 * stations, at + 1)), (2 * stations, LANES)
            )
            imag = jnp.broadcast_to(
                lax.slice(column, (0, pairs + at), (2 * stations, pairs + at + 1)),
                (2 * stations, LANES),
            )
            one = lax.slice(row_values[0], (at, 0), (at + 1, LANES))
            two = lax.slice(row_values[1], (at, 0), (at + 1, LANES))
            out[b, f] = (real * one + imag * two).astype(BF16)
        copy = pltpu.make_async_copy(out.at[b], out_hbm.at[b], sems.at[b])
        copy.start()
        ends.append(copy)
    for copy in ends:
        copy.wait()


VMEM_SPEC = pl.BlockSpec(memory_space=pltpu.VMEM)
SMEM_SPEC = pl.BlockSpec(memory_space=pltpu.SMEM)
ANY_SPEC = pl.BlockSpec(memory_space=pl.ANY)


def front(sections, stations, starts, section, owner_map, taper, voltages, beam_weight_table):
    inputs = voltages.shape[1]
    taps, length = taper.shape
    frames = voltages.shape[2] // length - taps + 1
    channels = length // 2
    chunks = channels // LANES
    weights = jnp.transpose(beam_weight_table[0], (0, 2, 1, 3))
    dims = (inputs, taps, frames, length, weights.shape[0], sections, stations)
    return pl.pallas_call(
        functools.partial(front_kernel, dims),
        out_shape=jax.ShapeDtypeStruct((sections, channels // sections, LANES), BF16),
        in_specs=[SMEM_SPEC, SMEM_SPEC, VMEM_SPEC, VMEM_SPEC, ANY_SPEC, ANY_SPEC, ANY_SPEC],
        out_specs=VMEM_SPEC,
        scratch_shapes=[
            pltpu.VMEM((inputs, voltages.shape[2]), BF16),
            pltpu.VMEM(weights.shape, BF16),
            pltpu.VMEM((chunks, length, 2 * LANES), BF16),
            pltpu.VMEM((frames * inputs, length), BF16),
            pltpu.VMEM((LANES, channels), F32),
            pltpu.SemaphoreType.DMA((inputs // 16 + chunks + 1,)),
        ],
        name="front",
    )(
        starts, section, owner_map.reshape(1, channels), taper, voltages, weights,
        jnp.asarray(dft_table(length)),
    )


def back(beam_count, frames, z):
    stations = z.shape[0]
    shape = (beam_count, frames, 2 * stations, 4 * stations)
    matrices = [jnp.asarray(m) for m in selectors(beam_count, frames, stations)]
    return pl.pallas_call(
        functools.partial(back_kernel, (beam_count, frames, stations)),
        out_shape=jax.ShapeDtypeStruct(shape, BF16),
        in_specs=[VMEM_SPEC] * 5,
        out_specs=ANY_SPEC,
        scratch_shapes=[pltpu.VMEM(shape, BF16), pltpu.SemaphoreType.DMA((beam_count,))],
        name="back",
    )(z, *matrices)


def local(voltages, taper, beam_weight_table, starts, owner_map):
    sections = lax.axis_size("section")
    stations = lax.axis_size("station")
    section = lax.axis_index("section").astype(jnp.int32).reshape(1)
    partial = front(
        sections, stations, starts, section, owner_map, taper, voltages, beam_weight_table
    )
    arrived = lax.all_to_all(partial, "section", split_axis=0, concat_axis=0, tiled=True)
    complete = jnp.sum(arrived.astype(F32), axis=0)
    z = lax.all_to_all(
        complete.reshape(stations, 1, LANES), "station", split_axis=0, concat_axis=0, tiled=True
    ).reshape(stations, LANES)
    beam_count = beam_weight_table.shape[1]
    frames = voltages.shape[2] // taper.shape[1] - taper.shape[0] + 1
    visible = back(beam_count, frames, z)
    return visible.reshape(1, 1, 1, *visible.shape)


def solution(mesh):
    placed = (
        P("station", "section", None),
        P(),
        P("station", None, "section", None, None),
        P(),
        P(),
    )
    return jax.shard_map(
        local,
        mesh=mesh,
        in_specs=placed,
        out_specs=P("section", "station", None, None, None, None, None),
        check_vma=False,
    )
```

time: 304 us -> 55.7 us (0.18)
  waiting for transfers between devices: 205 us -> 0 us
  other arithmetic: 39.3 us -> 0.02 us
  blocking collectives: 23.5 us -> 45.5 us
  local copies, waits for them, and re-layouts: 16 us -> 1.91 us
  between operations: 13.6 us -> 0.01 us
  Pallas kernels: 0 us -> 7.9 us
  matrix products: 5.93 us -> 0 us
    psum x1 -> x0, waiting for transfers between devices: 133 us -> none  [spread(): return lax.psum(block, axis)]
    all_gather x1 -> x0, waiting for transfers between devices: 72 us -> none  [prefix(): pieces = lax.all_gather(value, axis)]
    all_to_all x1 -> x2, blocking collectives: 23.5 us -> 45.5 us  [the longest x1 27.7 us: local(): lax.all_to_all(partial, 'section', split_axis=0, concat_axis=0, tiled=True)]
    select_n x18 -> x0, other arithmetic: 16.1 us -> none  [the longest x15 15.4 us: turn(): return jnp.where(position < mine, longer, subtotal)]
    another operation x3 -> x0, other arithmetic: 12.2 us -> none
    pallas_call x0 -> x2, Pallas kernels: none -> 7.9 us  [the longest x1 5.21 us: front(): pl.pallas_call(functools.partial(front_kernel, dims), out_shape=jax.Shape...]
    another operation x8 -> x0, local copies, waits for them, and re-layouts: 6.44 us -> none  [the longest x1 3.45 us: local(): jnp.stack([real_b, imag_b], axis=3)]
    dot_general x5 -> x0, matrix products: 5.93 us -> none  [the longest x1 1.28 us: local(): jnp.einsum('bapk,apfk->kbpf', real_w, imag_x)]
  transfers between devices with their start and end apart: 2 -> 0, of which waited for: 2 -> 0; matrix products, arithmetic and copies ran while one was open for 1% -> 0% of each run, Pallas kernels for 0% -> 0%
where the time goes in v1:
time: 55.7 us; the launch traced here: 55.3 us
  blocking collectives  45.5 us (82%)
  Pallas kernels  7.9 us (14%)
  local copies, waits for them, and re-layouts  1.91 us (3%)
    all_to_all x1, blocking collectives, local(): lax.all_to_all(partial, 'section', split_axis=0, concat_axis=0, tiled=True)  27.7 us
    all_to_all x1, blocking collectives, local(): lax.all_to_all(complete.reshape(stations, 1, LANES), 'station', split_axi...  17.8 us
    pallas_call x1, Pallas kernels, front(): pl.pallas_call(functools.partial(front_kernel, dims), out_shape=jax.Shape...  5.21 us
    pallas_call x1, Pallas kernels, back(): pl.pallas_call(functools.partial(back_kernel, (beam_count, frames, statio...  2.7 us
    unnamed x1, local copies, waits for them, and re-layouts  1.91 us

profile of v1, /device:TPU:1, one launch (start us, length us, event | category | flops | bytes accessed | tf_op | source)
XLA Modules:
  0.0 55.3 jit_solution(9812422627485768664)
XLA Ops:
  0.0 1.9 %copy.14 = bf16[1,8,32,2,512]{4,2,3,1,0:T(8,128)(2,1)} copy(bf16[1,8,32,2,512]{4,3,2,1,0:T(2,128)(2,1)} %param.12) | data formatting | bytes 1048576 | tf_op args[2]
  1.9 5.2 %front.1 = bf16[16,32,128]{2,1,0:T(8,128)(2,1)} custom-call(s32[8]{0:T(128)} %starts_ref.1, s32[1]{0:T(128)} %bitcast.section_ref, s32[1,512]{1,0:T(1,128)} %bitcast.13, f32[14,1024]{1,0:T(8,128)} %taper_ref.1, bf16[1,32,17408]{2,1,0:T(8,128)(2,1)} %volts_hbm.1, bf16[8,2,32,512]{3,2,1,0:T(8,128)(2,1)} %bitcast.10, bf16[1024,1024]{1,0:T(8,128)(2,1)} %constant.16.clone.table_hbm), custom_call_target="tpu_custom_call" | custom-call | tf_op jit(solution)/shard_map/front/pallas_call | solution.py:228
  7.1 27.7 %all_to_all.10 = bf16[16,32,128]{2,1,0:T(8,128)(2,1)S(1)} all-to-all(bf16[16,32,128]{2,1,0:T(8,128)(2,1)} %front.1), channel_id=1, replica_groups=mesh['station'=32,'section'=16] {'section'}, dimensions={0} | all-to-all | bytes 262144 | tf_op jit(solution)/shard_map/all_to_all | solution.py:269
  34.9 17.8 %all_to_all.11 = f32[32,1,128]{2,1,0:T(1,128)} all-to-all(f32[32,1,128]{2,1,0:T(1,128)S(1)} %bitcast.12), channel_id=1, replica_groups=mesh['station'=32,'section'=16] {'station'}, dimensions={0} | all-to-all | bytes 32768 | tf_op jit(solution)/shard_map/all_to_all | solution.py:271
  52.6 2.7 %back.1 = bf16[8,4,64,128]{3,2,1,0:T(8,128)(2,1)} custom-call(f32[32,128]{1,0:T(8,128)} %bitcast.11, bf16[128,128]{1,0:T(8,128)(2,1)} %constant.17.clone.pick_ref, bf16[2,128,64]{2,1,0:T(8,128)(2,1)} %constant.18.clone.columns_ref, bf16[2,64,32]{2,1,0:T(8,128)(2,1)} %constant.19.clone.spread_ref, bf16[2,2,2,32,128]{4,3,2,1,0:T(8,128)(2,1)} %constant.20.clone.rows_ref), custom_call_target="tpu_custom_call" | custom-call | tf_op jit(solution)/shard_map/back/pallas_call | solution.py:252
  (1 shorter events, 0.0 us)

commit v2 on v1

--- a/solution.py
+++ b/solution.py
@@ -27,8 +27,8 @@
 
 
 def front_kernel(
-    dims, starts_ref, section_ref, owner_ref, taper_ref, volts_hbm, weights_hbm, table_hbm,
-    out_ref, volts, weights, table, rows, beams, sems,
+    dims, section_ref, starts_hbm, owner_hbm, taper_hbm, volts_hbm, weights_hbm, table_hbm,
+    out_ref, starts, owner, taper, volts, weights, table, rows, gain, mixed, beams, sems,
 ):
     inputs, taps, frames, length, beam_count, sections, stations = dims
     channels = length // 2
@@ -36,29 +36,33 @@
     block = channels // sections
     half = 16
     parts = inputs // half
+    starts_copy = pltpu.make_async_copy(starts_hbm, starts, sems.at[0])
+    owner_copy = pltpu.make_async_copy(owner_hbm, owner, sems.at[1])
+    taper_copy = pltpu.make_async_copy(taper_hbm, taper, sems.at[2])
+    weight_copy = pltpu.make_async_copy(weights_hbm.at[0], weights, sems.at[3])
     volt_copies = [
         pltpu.make_async_copy(
-            volts_hbm.at[0, pl.ds(i * half, half)], volts.at[pl.ds(i * half, half)], sems.at[i]
+            volts_hbm.at[0, pl.ds(i * half, half)], volts.at[pl.ds(i * half, half)], sems.at[4 + i]
         )
         for i in range(parts)
     ]
     table_copies = [
         pltpu.make_async_copy(
-            table_hbm.at[:, pl.ds(c * 2 * LANES, 2 * LANES)], table.at[c], sems.at[parts + c]
+            table_hbm.at[:, pl.ds(c * 2 * LANES, 2 * LANES)], table.at[c], sems.at[4 + parts + c]
         )
         for c in range(chunks)
     ]
-    weight_copy = pltpu.make_async_copy(weights_hbm, weights, sems.at[parts + chunks])
-    for copy in volt_copies + table_copies:
+    copies = [taper_copy, *volt_copies, *table_copies[:1], weight_copy, *table_copies[1:]]
+    for copy in copies + [starts_copy, owner_copy]:
         copy.start()
-    weight_copy.start()
-
+
+    taper_copy.wait()
     for i in range(parts):
         volt_copies[i].wait()
         for c in range(length // LANES):
             at = c * LANES
-            taper = [
-                jnp.broadcast_to(taper_ref[pl.ds(t, 1), pl.ds(at, LANES)], (half, LANES))
+            gains = [
+                jnp.broadcast_to(taper[pl.ds(t, 1), pl.ds(at, LANES)], (half, LANES))
                 for t in range(taps)
             ]
             sums = [None] * frames
@@ -67,64 +71,64 @@
                 for f in range(frames):
                     t = g - f
                     if 0 <= t < taps:
-                        term = taper[t] * value
+                        term = gains[t] * value
                         sums[f] = term if sums[f] is None else sums[f] + term
             for f in range(frames):
                 rows[pl.ds(f * inputs + i * half, half), pl.ds(at, LANES)] = sums[f].astype(BF16)
 
+    starts_copy.wait()
     section = section_ref[0]
     keep = [
-        jnp.where(((section - starts_ref[b] + sections) & (sections - 1)) < sections // 2, 1.0, 0.0)
+        jnp.where(((section - starts[b] + sections) & (sections - 1)) < sections // 2, 1.0, 0.0)
         for b in range(beam_count)
     ]
     row = lax.broadcasted_iota(jnp.int32, (8, LANES), 0)
     low = row < 4
-    first = (row & 2) == 0
-    tiles = inputs // 8
-
-    def tile_of(array, start):
-        return lax.slice(array, (start, 0), (start + 8, LANES))
-
-    for c in range(chunks):
+    even = (row & 1) == 0
+    tiles = 2 * inputs // 8
+
+    def spectra_of(c):
         table_copies[c].wait()
         spectra = jnp.dot(rows[...], table[c], preferred_element_type=F32)
-        real_x = lax.slice(spectra, (0, 0), (frames * inputs, LANES))
-        imag_x = lax.slice(spectra, (0, LANES), (frames * inputs, 2 * LANES))
-        if c == 0:
-            weight_copy.wait()
+        for f in range(frames):
+            real = lax.slice(spectra, (f * inputs, 0), ((f + 1) * inputs, LANES))
+            imag = lax.slice(spectra, (f * inputs, LANES), ((f + 1) * inputs, 2 * LANES))
+            for at, one, two in ((0, real, -imag), (1, imag, real)):
+                mixed[c % 2, at, f, pl.ds(0, inputs, stride=2), :] = one
+                mixed[c % 2, at, f, pl.ds(1, inputs, stride=2), :] = two
+
+    spectra_of(0)
+    weight_copy.wait()
+    for b in range(beam_count):
+        gain[b] = weights[b].astype(F32).reshape(2 * inputs, channels)
+    for c in range(chunks):
+        if c + 1 < chunks:
+            spectra_of(c + 1)
         for b in range(beam_count):
-            real_w = weights[b, 0, :, pl.ds(c * LANES, LANES)].astype(F32)
-            imag_w = weights[b, 1, :, pl.ds(c * LANES, LANES)].astype(F32)
-            sums = [[], []]
-            for f in range(frames):
-                real = imag = None
-                for i in range(tiles):
-                    xr = tile_of(real_x, f * inputs + i * 8)
-                    xi = tile_of(imag_x, f * inputs + i * 8)
-                    wr = tile_of(real_w, i * 8)
-                    wi = tile_of(imag_w, i * 8)
-                    re = wr * xr - wi * xi
-                    im = wr * xi + wi * xr
-                    real = re if real is None else real + re
-                    imag = im if imag is None else imag + im
-                sums[0].append(real)
-                sums[1].append(imag)
+            gains = [gain[b, pl.ds(8 * i, 8), pl.ds(c * LANES, LANES)] for i in range(tiles)]
             for part in range(2):
-                v = sums[part]
+                v = []
+                for f in range(frames):
+                    total = None
+                    for i in range(tiles):
+                        term = gains[i] * mixed[c % 2, part, f, pl.ds(8 * i, 8), :]
+                        total = term if total is None else total + term
+                    v.append(total)
                 pairs = []
                 for one, two in ((v[0], v[1]), (v[2], v[3])):
                     pairs.append(
                         jnp.where(low, one, two) + pltpu.roll(jnp.where(low, two, one), 4, 0)
                     )
-                one = pairs[0] + pltpu.roll(pairs[0], 6, 0)
-                two = pairs[1] + pltpu.roll(pairs[1], 2, 0)
+                one = pairs[0] + pltpu.roll(pairs[0], 7, 0)
+                two = pairs[1] + pltpu.roll(pairs[1], 1, 0)
                 beams[pl.ds(b * 16 + part * 8, 8), pl.ds(c * LANES, LANES)] = (
-                    jnp.where(first, one, two) * keep[b]
+                    jnp.where(even, one, two) * keep[b]
                 )
 
+    owner_copy.wait()
     per = LANES // block
     for c in range(chunks):
-        owners = owner_ref[pl.ds(0, 1), pl.ds(c * LANES, LANES)]
+        owners = owner[pl.ds(0, 1), pl.ds(c * LANES, LANES)]
         lane = lax.broadcasted_iota(jnp.int32, (1, LANES), 1)
         target = (lane // block) * block + owners
         slot = lax.broadcasted_iota(jnp.int32, (LANES, LANES), 0)
@@ -138,7 +142,7 @@
 
 
 def place_of(beam, frame, part, pol):
-    return beam * 16 + part * 8 + (frame & 1) * 4 + (frame >> 1) * 2 + pol
+    return beam * 16 + part * 8 + (frame & 1) * 4 + pol * 2 + (frame >> 1)
 
 
 def selectors(beam_count, frames, stations):
@@ -214,7 +218,7 @@
 
 VMEM_SPEC = pl.BlockSpec(memory_space=pltpu.VMEM)
 SMEM_SPEC = pl.BlockSpec(memory_space=pltpu.SMEM)
-ANY_SPEC = pl.BlockSpec(memory_space=pl.ANY)
+HBM_SPEC = pl.BlockSpec(memory_space=pltpu.HBM)
 
 
 def front(sections, stations, starts, section, owner_map, taper, voltages, beam_weight_table):
@@ -223,25 +227,36 @@
     frames = voltages.shape[2] // length - taps + 1
     channels = length // 2
     chunks = channels // LANES
-    weights = jnp.transpose(beam_weight_table[0], (0, 2, 1, 3))
-    dims = (inputs, taps, frames, length, weights.shape[0], sections, stations)
+    dims = (inputs, taps, frames, length, beam_weight_table.shape[1], sections, stations)
     return pl.pallas_call(
         functools.partial(front_kernel, dims),
         out_shape=jax.ShapeDtypeStruct((sections, channels // sections, LANES), BF16),
-        in_specs=[SMEM_SPEC, SMEM_SPEC, VMEM_SPEC, VMEM_SPEC, ANY_SPEC, ANY_SPEC, ANY_SPEC],
+        in_specs=[SMEM_SPEC] + [HBM_SPEC] * 6,
         out_specs=VMEM_SPEC,
         scratch_shapes=[
+            pltpu.SMEM(starts.shape, jnp.int32),
+            pltpu.VMEM((1, channels), jnp.int32),
+            pltpu.VMEM(taper.shape, F32),
             pltpu.VMEM((inputs, voltages.shape[2]), BF16),
-            pltpu.VMEM(weights.shape, BF16),
+            pltpu.VMEM(beam_weight_table.shape[1:], BF16),
             pltpu.VMEM((chunks, length, 2 * LANES), BF16),
             pltpu.VMEM((frames * inputs, length), BF16),
+            pltpu.VMEM((beam_weight_table.shape[1], 2 * inputs, channels), F32),
+            pltpu.VMEM((2, 2, frames, 2 * inputs, LANES), F32),
             pltpu.VMEM((LANES, channels), F32),
-            pltpu.SemaphoreType.DMA((inputs // 16 + chunks + 1,)),
+            pltpu.SemaphoreType.DMA((4 + inputs // 16 + chunks,)),
         ],
+        compiler_params=pltpu.CompilerParams(vmem_limit_bytes=16 << 20),
         name="front",
     )(
-        starts, section, owner_map.reshape(1, channels), taper, voltages, weights,
-        jnp.asarray(dft_table(length)),
+        section,
+        *[
+            pltpu.with_memory_space_constraint(array, pltpu.HBM)
+            for array in (
+                starts, owner_map.reshape(1, channels), taper, voltages, beam_weight_table,
+                jnp.asarray(dft_table(length)),
+            )
+        ],
     )
 
 
@@ -253,8 +268,9 @@
         functools.partial(back_kernel, (beam_count, frames, stations)),
         out_shape=jax.ShapeDtypeStruct(shape, BF16),
         in_specs=[VMEM_SPEC] * 5,
-        out_specs=ANY_SPEC,
+        out_specs=HBM_SPEC,
         scratch_shapes=[pltpu.VMEM(shape, BF16), pltpu.SemaphoreType.DMA((beam_count,))],
+        compiler_params=pltpu.CompilerParams(vmem_limit_bytes=16 << 20),
         name="back",
     )(z, *matrices)
 

time: 55.7 us -> 51 us (0.916)
  Pallas kernels: 7.9 us -> 5.62 us
  local copies, waits for them, and re-layouts: 1.91 us -> 0.02 us
    unnamed x1 -> x8, local copies, waits for them, and re-layouts: 1.91 us -> 0.02 us
    pallas_call x1, Pallas kernels: 5.21 us -> 3.85 us  [front(): pl.pallas_call(functools.partial(front_kernel, dims), out_shape=jax.Shape...]
    pallas_call x1, Pallas kernels: 2.7 us -> 1.77 us  [back(): pl.pallas_call(functools.partial(back_kernel, (beam_count, frames, statio...]
where the time goes in v2:
time: 51 us; the launch traced here: 50.8 us
  blocking collectives  45.1 us (88%)
  Pallas kernels  5.62 us (11%)
    all_to_all x1, blocking collectives, local(): lax.all_to_all(partial, 'section', split_axis=0, concat_axis=0, tiled=True)  27.5 us
    all_to_all x1, blocking collectives, local(): lax.all_to_all(complete.reshape(stations, 1, LANES), 'station', split_axi...  17.6 us
    pallas_call x1, Pallas kernels, front(): pl.pallas_call(functools.partial(front_kernel, dims), out_shape=jax.Shape...  3.85 us
    pallas_call x1, Pallas kernels, back(): pl.pallas_call(functools.partial(back_kernel, (beam_count, frames, statio...  1.77 us

profile of v2, /device:TPU:1, one launch (start us, length us, event | category | flops | bytes accessed | tf_op | source)
XLA Modules:
  0.0 50.8 jit_solution(2668568046232611228)
XLA Ops:
  0.0 0.0 copy-start
  0.0 0.0 copy-start.1
  0.0 0.0 copy-start.2
  0.0 0.0 copy-start.3
  0.0 3.9 %front.1 = bf16[16,32,128]{2,1,0:T(8,128)(2,1)S(1)} custom-call(s32[1]{0:T(128)} %bitcast.section_ref, s32[8]{0:T(128)} %starts_hbm.1, s32[1,512]{1,0:T(1,128)} %bitcast.7, f32[14,1024]{1,0:T(8,128)} %taper_hbm.1, bf16[1,32,17408]{2,1,0:T(8,128)(2,1)} %volts_hbm.1, bf16[1,8,32,2,512]{4,3,2,1,0:T(2,128)(2,1)} %weights_hbm.1, ...), custom_call_target="tpu_custom_call" | custom-call | tf_op jit(solution)/shard_map/front/pallas_call | solution.py:231
  3.9 27.5 %all_to_all.10 = bf16[16,32,128]{2,1,0:T(8,128)(2,1)S(1)} all-to-all(bf16[16,32,128]{2,1,0:T(8,128)(2,1)S(1)} %front.1), channel_id=1, replica_groups=mesh['station'=32,'section'=16] {'section'}, dimensions={0} | all-to-all | bytes 262144 | tf_op jit(solution)/shard_map/all_to_all | solution.py:285
  31.4 17.6 %all_to_all.11 = f32[32,1,128]{2,1,0:T(1,128)S(1)} all-to-all(f32[32,1,128]{2,1,0:T(1,128)S(1)} %bitcast.6), channel_id=1, replica_groups=mesh['station'=32,'section'=16] {'station'}, dimensions={0} | all-to-all | bytes 32768 | tf_op jit(solution)/shard_map/all_to_all | solution.py:287
  49.0 0.0 copy-done
  49.0 0.0 copy-done.1
  49.1 0.0 copy-done.2
  49.1 0.0 copy-done.3
  49.1 1.8 %back.1 = bf16[8,4,64,128]{3,2,1,0:T(8,128)(2,1)} custom-call(f32[32,128]{1,0:T(8,128)S(1)} %bitcast.5, bf16[128,128]{1,0:T(8,128)(2,1)S(1)} %copy-done.3, bf16[2,128,64]{2,1,0:T(8,128)(2,1)S(1)} %copy-done.1, bf16[2,64,32]{2,1,0:T(8,128)(2,1)S(1)} %copy-done.2, bf16[2,2,2,32,128]{4,3,2,1,0:T(8,128)(2,1)S(1)} %copy-done), custom_call_target="tpu_custom_call" | custom-call | tf_op jit(solution)/shard_map/back/pallas_call | solution.py:267
  (1 shorter events, 0.0 us)
Async XLA Ops:
  0.0 49.0 %copy-start = (bf16[2,2,2,32,128]{4,3,2,1,0:T(8,128)(2,1)S(1)}, bf16[2,2,2,32,128]{4,3,2,1,0:T(8,128)(2,1)}, u32[]{:S(2)}) copy-start(bf16[2,2,2,32,128]{4,3,2,1,0:T(8,128)(2,1)} %constant.20.clone.rows_ref) | copy-start | bytes 196612
  0.0 49.0 %copy-start.1 = (bf16[2,128,64]{2,1,0:T(8,128)(2,1)S(1)}, bf16[2,128,64]{2,1,0:T(8,128)(2,1)}, u32[]{:S(2)}) copy-start(bf16[2,128,64]{2,1,0:T(8,128)(2,1)} %constant.18.clone.columns_ref) | copy-start | bytes 98308
  0.0 49.0 %copy-start.2 = (bf16[2,64,32]{2,1,0:T(8,128)(2,1)S(1)}, bf16[2,64,32]{2,1,0:T(8,128)(2,1)}, u32[]{:S(2)}) copy-start(bf16[2,64,32]{2,1,0:T(8,128)(2,1)} %constant.19.clone.spread_ref) | copy-start | bytes 24580
  0.0 49.0 %copy-start.3 = (bf16[128,128]{1,0:T(8,128)(2,1)S(1)}, bf16[128,128]{1,0:T(8,128)(2,1)}, u32[]{:S(2)}) copy-start(bf16[128,128]{1,0:T(8,128)(2,1)} %constant.17.clone.pick_ref) | copy-start | bytes 98308

commit v3 on v2

--- a/solution.py
+++ b/solution.py
@@ -28,7 +28,7 @@
 
 def front_kernel(
     dims, section_ref, starts_hbm, owner_hbm, taper_hbm, volts_hbm, weights_hbm, table_hbm,
-    out_ref, starts, owner, taper, volts, weights, table, rows, gain, mixed, beams, sems,
+    out_ref, starts, owner, taper, volts, weights, table, rows, gain, mixed, beams, turned, sems,
 ):
     inputs, taps, frames, length, beam_count, sections, stations = dims
     channels = length // 2
@@ -52,7 +52,7 @@
         )
         for c in range(chunks)
     ]
-    copies = [taper_copy, *volt_copies, *table_copies[:1], weight_copy, *table_copies[1:]]
+    copies = [taper_copy, *volt_copies, weight_copy, *table_copies]
     for copy in copies + [starts_copy, owner_copy]:
         copy.start()
 
@@ -97,10 +97,14 @@
                 mixed[c % 2, at, f, pl.ds(0, inputs, stride=2), :] = one
                 mixed[c % 2, at, f, pl.ds(1, inputs, stride=2), :] = two
 
-    spectra_of(0)
     weight_copy.wait()
     for b in range(beam_count):
         gain[b] = weights[b].astype(F32).reshape(2 * inputs, channels)
+    owner_copy.wait()
+    spectra_of(0)
+    per = LANES // block
+    lane = lax.broadcasted_iota(jnp.int32, (1, LANES), 1)
+    slot = lax.broadcasted_iota(jnp.int32, (LANES, LANES), 0)
     for c in range(chunks):
         if c + 1 < chunks:
             spectra_of(c + 1)
@@ -121,24 +125,27 @@
                     )
                 one = pairs[0] + pltpu.roll(pairs[0], 7, 0)
                 two = pairs[1] + pltpu.roll(pairs[1], 1, 0)
-                beams[pl.ds(b * 16 + part * 8, 8), pl.ds(c * LANES, LANES)] = (
+                beams[c, pl.ds(b * 16 + part * 8, 8), :] = (
                     jnp.where(even, one, two) * keep[b]
                 )
 
-    owner_copy.wait()
-    per = LANES // block
-    for c in range(chunks):
         owners = owner[pl.ds(0, 1), pl.ds(c * LANES, LANES)]
-        lane = lax.broadcasted_iota(jnp.int32, (1, LANES), 1)
-        target = (lane // block) * block + owners
-        slot = lax.broadcasted_iota(jnp.int32, (LANES, LANES), 0)
-        pick = jnp.where(slot == target, 1.0, 0.0).astype(BF16)
-        values = beams[:, pl.ds(c * LANES, LANES)].astype(BF16)
+        pick = jnp.where(slot == (lane // block) * block + owners, 1.0, 0.0).astype(BF16)
         placed = lax.dot_general(
-            pick, values, (((1,), (1,)), ((), ())), preferred_element_type=F32
-        ).astype(BF16)
+            pick, beams[c].astype(BF16), (((1,), (1,)), ((), ())), preferred_element_type=F32
+        )
         for s in range(per):
-            out_ref[c * per + s] = lax.slice(placed, (s * block, 0), ((s + 1) * block, LANES))
+            turned[pl.ds(c * per + s, stations, stride=sections), :] = lax.slice(
+                placed, (s * block, 0), ((s + 1) * block, LANES)
+            )
+    out_ref[...] = turned[...].astype(BF16).reshape(stations, sections, LANES)
+
+
+def turn_kernel(in_ref, out_ref, rows):
+    first, second, _ = in_ref.shape
+    rows[...] = in_ref[...].astype(F32).reshape(first * second, LANES)
+    for i in range(second):
+        out_ref[i] = rows[pl.ds(i, first, stride=second), :].astype(BF16)
 
 
 def place_of(beam, frame, part, pol):
@@ -146,72 +153,70 @@
 
 
 def selectors(beam_count, frames, stations):
-    pairs = beam_count * frames
-    pick = np.zeros((4 * pairs, LANES), np.float32)
-    columns = np.zeros((2, LANES, 2 * pairs), np.float32)
+    count = beam_count * frames * 2
+    group = count // 4
+    pick = np.zeros((2, 2, count, LANES), np.float32)
+    columns = np.zeros((4, 2, LANES, group), np.float32)
     for b in range(beam_count):
         for f in range(frames):
             for part in range(2):
+                at = (b * frames + f) * 2 + part
                 for pol in range(2):
                     j = place_of(b, f, part, pol)
-                    pick[(part * 2 + pol) * pairs + b * frames + f, j] = 1
-                    columns[pol, j, part * pairs + b * frames + f] = 1
+                    pick[0, pol, at, j] = 1
+                    pick[1, pol, at, place_of(b, f, 1 - part, pol)] = 1 if part else -1
+                    columns[at // group, pol, j, at % group] = 1
     spread = np.zeros((2, stations, 2 * stations), np.float32)
     for st in range(stations):
         for pol in range(2):
             spread[pol, st, 2 * st + pol] = 1
     zero = np.zeros_like(spread)
-    left = np.concatenate([spread, zero], axis=2)
-    right = np.concatenate([zero, spread], axis=2)
-    first = np.stack([left, -right])
-    second = np.stack([right, left])
-    rows = np.stack([first, second])
-    as_type = lambda a: a.astype(ml_dtypes.bfloat16)
-    return as_type(pick), as_type(columns), as_type(np.swapaxes(spread, 1, 2)), as_type(rows)
-
-
-def back_kernel(dims, z_ref, pick_ref, columns_ref, spread_ref, rows_ref, out_hbm, out, sems):
+    rows = np.stack([np.concatenate([spread, zero], 2), np.concatenate([zero, spread], 2)])
+    arrays = (pick.reshape(4 * count, LANES), columns, np.swapaxes(spread, 1, 2), rows)
+    return [a.astype(ml_dtypes.bfloat16) for a in arrays]
+
+
+def back_kernel(dims, parts_ref, pick_ref, columns_ref, spread_ref, rows_ref, out_hbm, out, sems):
     beam_count, frames, stations = dims
-    pairs = beam_count * frames
-    z = z_ref[...].astype(BF16)
+    count = beam_count * frames * 2
+    group = count // 4
+    total = parts_ref[0].astype(F32)
+    for i in range(1, parts_ref.shape[0]):
+        total = total + parts_ref[i].astype(F32)
+    z = total.astype(BF16)
     turned = lax.dot_general(
         pick_ref[...], z, (((1,), (1,)), ((), ())), preferred_element_type=F32
     ).astype(BF16)
-    row_values = []
-    for kind in range(2):
-        total = None
-        for part in range(2):
-            for pol in range(2):
-                at = (part * 2 + pol) * pairs
-                term = jnp.dot(
-                    lax.slice(turned, (at, 0), (at + pairs, stations)),
-                    rows_ref[kind, part, pol],
-                    preferred_element_type=F32,
-                )
-                total = term if total is None else total + term
-        row_values.append(total)
-    column = None
-    for pol in range(2):
-        chosen = jnp.dot(z, columns_ref[pol], preferred_element_type=F32).astype(BF16)
-        term = jnp.dot(spread_ref[pol], chosen, preferred_element_type=F32)
-        column = term if column is None else column + term
+    right = None
+    for side in range(2):
+        for pol in range(2):
+            at = (side * 2 + pol) * count
+            term = jnp.dot(
+                lax.slice(turned, (at, 0), (at + count, stations)), rows_ref[side, pol],
+                preferred_element_type=F32,
+            )
+            right = term if right is None else right + term
+    pair = lax.broadcasted_iota(jnp.int32, (group, LANES), 0) // 2
     ends = []
-    for b in range(beam_count):
-        for f in range(frames):
-            at = b * frames + f
-            real = jnp.broadcast_to(
-                lax.slice(column, (0, at), (2 * stations, at + 1)), (2 * stations, LANES)
-            )
-            imag = jnp.broadcast_to(
-                lax.slice(column, (0, pairs + at), (2 * stations, pairs + at + 1)),
-                (2 * stations, LANES),
-            )
-            one = lax.slice(row_values[0], (at, 0), (at + 1, LANES))
-            two = lax.slice(row_values[1], (at, 0), (at + 1, LANES))
-            out[b, f] = (real * one + imag * two).astype(BF16)
-        copy = pltpu.make_async_copy(out.at[b], out_hbm.at[b], sems.at[b])
-        copy.start()
-        ends.append(copy)
+    for g in range(4):
+        left = None
+        for pol in range(2):
+            chosen = jnp.dot(z, columns_ref[g, pol], preferred_element_type=F32).astype(BF16)
+            term = jnp.dot(spread_ref[pol], chosen, preferred_element_type=F32)
+            left = term if left is None else left + term
+        left = left.astype(BF16)
+        mine = lax.slice(right, (g * group, 0), ((g + 1) * group, LANES))
+        spaced = jnp.concatenate(
+            [jnp.where(pair == i, mine, 0.0).astype(BF16) for i in range(group // 2)], axis=1
+        )
+        product = jnp.dot(left, spaced, preferred_element_type=F32).astype(BF16)
+        for i in range(group // 2):
+            b, f = divmod(g * (group // 2) + i, frames)
+            out[b, f] = lax.slice(product, (0, i * LANES), (2 * stations, (i + 1) * LANES))
+            if f == frames - 1:
+                copy = pltpu.make_async_copy(out.at[b], out_hbm.at[b], sems.at[b])
+                copy.start()
+                ends.append(copy)
     for copy in ends:
         copy.wait()
 
@@ -230,7 +235,7 @@
     dims = (inputs, taps, frames, length, beam_weight_table.shape[1], sections, stations)
     return pl.pallas_call(
         functools.partial(front_kernel, dims),
-        out_shape=jax.ShapeDtypeStruct((sections, channels // sections, LANES), BF16),
+        out_shape=jax.ShapeDtypeStruct((channels // sections, sections, LANES), BF16),
         in_specs=[SMEM_SPEC] + [HBM_SPEC] * 6,
         out_specs=VMEM_SPEC,
         scratch_shapes=[
@@ -243,7 +248,8 @@
             pltpu.VMEM((frames * inputs, length), BF16),
             pltpu.VMEM((beam_weight_table.shape[1], 2 * inputs, channels), F32),
             pltpu.VMEM((2, 2, frames, 2 * inputs, LANES), F32),
-            pltpu.VMEM((LANES, channels), F32),
+            pltpu.VMEM((chunks, LANES, LANES), F32),
+            pltpu.VMEM((channels, LANES), F32),
             pltpu.SemaphoreType.DMA((4 + inputs // 16 + chunks,)),
         ],
         compiler_params=pltpu.CompilerParams(vmem_limit_bytes=16 << 20),
@@ -260,8 +266,21 @@
     )
 
 
-def back(beam_count, frames, z):
-    stations = z.shape[0]
+def turn(array):
+    first, second, _ = array.shape
+    return pl.pallas_call(
+        turn_kernel,
+        out_shape=jax.ShapeDtypeStruct((second, first, LANES), BF16),
+        in_specs=[VMEM_SPEC],
+        out_specs=VMEM_SPEC,
+        scratch_shapes=[pltpu.VMEM((first * second, LANES), F32)],
+        compiler_params=pltpu.CompilerParams(vmem_limit_bytes=4 << 20),
+        name="turn",
+    )(array)
+
+
+def back(beam_count, frames, parts):
+    stations = parts.shape[1]
     shape = (beam_count, frames, 2 * stations, 4 * stations)
     matrices = [jnp.asarray(m) for m in selectors(beam_count, frames, stations)]
     return pl.pallas_call(
@@ -272,24 +291,21 @@
         scratch_shapes=[pltpu.VMEM(shape, BF16), pltpu.SemaphoreType.DMA((beam_count,))],
         compiler_params=pltpu.CompilerParams(vmem_limit_bytes=16 << 20),
         name="back",
-    )(z, *matrices)
+    )(parts, *matrices)
 
 
 def local(voltages, taper, beam_weight_table, starts, owner_map):
     sections = lax.axis_size("section")
     stations = lax.axis_size("station")
     section = lax.axis_index("section").astype(jnp.int32).reshape(1)
-    partial = front(
+    parts = front(
         sections, stations, starts, section, owner_map, taper, voltages, beam_weight_table
     )
-    arrived = lax.all_to_all(partial, "section", split_axis=0, concat_axis=0, tiled=True)
-    complete = jnp.sum(arrived.astype(F32), axis=0)
-    z = lax.all_to_all(
-        complete.reshape(stations, 1, LANES), "station", split_axis=0, concat_axis=0, tiled=True
-    ).reshape(stations, LANES)
+    parts = lax.all_to_all(parts, "station", split_axis=0, concat_axis=0, tiled=True)
+    parts = lax.all_to_all(turn(parts), "section", split_axis=0, concat_axis=0, tiled=True)
     beam_count = beam_weight_table.shape[1]
     frames = voltages.shape[2] // taper.shape[1] - taper.shape[0] + 1
-    visible = back(beam_count, frames, z)
+    visible = back(beam_count, frames, parts)
     return visible.reshape(1, 1, 1, *visible.shape)
 
 

time: 51 us -> 50.1 us (0.982)
  the two profiles are of different devices: /device:TPU:1 before, /device:TPU:32 now
where the time goes in v3:
time: 50.1 us; the launch traced here: 49.9 us
  blocking collectives  43.9 us (88%)
  Pallas kernels  6 us (12%)
    all_to_all x1, blocking collectives, local(): lax.all_to_all(turn(parts), 'section', split_axis=0, concat_axis=0, tiled...  28.9 us
    all_to_all x1, blocking collectives, local(): lax.all_to_all(parts, 'station', split_axis=0, concat_axis=0, tiled=True)  15 us
    pallas_call x1, Pallas kernels, front(): pl.pallas_call(functools.partial(front_kernel, dims), out_shape=jax.Shape...  3.73 us
    pallas_call x1, Pallas kernels, back(): pl.pallas_call(functools.partial(back_kernel, (beam_count, frames, statio...  2.18 us

profile of v3, /device:TPU:32, one launch (start us, length us, event | category | flops | bytes accessed | tf_op | source)
XLA Modules:
  0.0 49.9 jit_solution(13106395991318673625)
XLA Ops:
  0.0 0.0 copy-start
  0.0 0.0 copy-start.1
  0.0 0.0 copy-start.2
  0.0 0.0 copy-start.3
  0.0 3.7 %front.1 = bf16[32,16,128]{2,1,0:T(8,128)(2,1)S(1)} custom-call(s32[1]{0:T(128)} %bitcast.section_ref, s32[8]{0:T(128)} %starts_hbm.1, s32[1,512]{1,0:T(1,128)} %bitcast.3, f32[14,1024]{1,0:T(8,128)} %taper_hbm.1, bf16[1,32,17408]{2,1,0:T(8,128)(2,1)} %volts_hbm.1, bf16[1,8,32,2,512]{4,3,2,1,0:T(2,128)(2,1)} %weights_hbm.1, ...), custom_call_target="tpu_custom_call" | custom-call | tf_op jit(solution)/shard_map/front/pallas_call | solution.py:236
  3.8 15.0 %all_to_all.10.in_ref = bf16[32,16,128]{2,1,0:T(8,128)(2,1)S(1)} all-to-all(bf16[32,16,128]{2,1,0:T(8,128)(2,1)S(1)} %front.1), channel_id=1, replica_groups=mesh['station'=32,'section'=16] {'station'}, dimensions={0} | all-to-all | bytes 262144 | tf_op jit(solution)/shard_map/all_to_all | solution.py:304
  18.7 0.1 turn.1
  18.8 28.9 %all_to_all.11.parts_ref = bf16[16,32,128]{2,1,0:T(8,128)(2,1)S(1)} all-to-all(bf16[16,32,128]{2,1,0:T(8,128)(2,1)S(1)} %turn.1), channel_id=1, replica_groups=mesh['station'=32,'section'=16] {'section'}, dimensions={0} | all-to-all | bytes 262144 | tf_op jit(solution)/shard_map/all_to_all | solution.py:305
  47.7 0.0 copy-done
  47.7 0.0 copy-done.1
  47.7 0.0 copy-done.2
  47.8 0.0 copy-done.3
  47.8 2.2 %back.1 = bf16[8,4,64,128]{3,2,1,0:T(8,128)(2,1)} custom-call(bf16[16,32,128]{2,1,0:T(8,128)(2,1)S(1)} %all_to_all.11.parts_ref, bf16[256,128]{1,0:T(8,128)(2,1)S(1)} %copy-done.1, bf16[4,2,128,16]{3,2,1,0:T(8,128)(2,1)S(1)} %copy-done, bf16[2,64,32]{2,1,0:T(8,128)(2,1)S(1)} %copy-done.3, bf16[2,2,32,128]{3,2,1,0:T(8,128)(2,1)S(1)} %copy-done.2), custom_call_target="tpu_custom_call" | custom-call | tf_op jit(solution)/shard_map/back/pallas_call | solution.py:286
Async XLA Ops:
  0.0 47.7 %copy-start = (bf16[4,2,128,16]{3,2,1,0:T(8,128)(2,1)S(1)}, bf16[4,2,128,16]{3,2,1,0:T(8,128)(2,1)}, u32[]{:S(2)}) copy-start(bf16[4,2,128,16]{3,2,1,0:T(8,128)(2,1)} %constant.16.clone.columns_ref) | copy-start | bytes 98308
  0.0 47.7 %copy-start.1 = (bf16[256,128]{1,0:T(8,128)(2,1)S(1)}, bf16[256,128]{1,0:T(8,128)(2,1)}, u32[]{:S(2)}) copy-start(bf16[256,128]{1,0:T(8,128)(2,1)} %constant.15.clone.pick_ref) | copy-start | bytes 196612
  0.0 47.7 %copy-start.2 = (bf16[2,2,32,128]{3,2,1,0:T(8,128)(2,1)S(1)}, bf16[2,2,32,128]{3,2,1,0:T(8,128)(2,1)}, u32[]{:S(2)}) copy-start(bf16[2,2,32,128]{3,2,1,0:T(8,128)(2,1)} %constant.18.clone.rows_ref) | copy-start | bytes 98308
  0.0 47.7 %copy-start.3 = (bf16[2,64,32]{2,1,0:T(8,128)(2,1)S(1)}, bf16[2,64,32]{2,1,0:T(8,128)(2,1)}, u32[]{:S(2)}) copy-start(bf16[2,64,32]{2,1,0:T(8,128)(2,1)} %constant.17.clone.spread_ref) | copy-start | bytes 24580

commit v4 on v3

--- a/solution.py
+++ b/solution.py
@@ -11,29 +11,33 @@
 from jax.sharding import PartitionSpec as P
 
 LANES = 128
+DEPTH = 256
 F32 = jnp.float32
 BF16 = jnp.bfloat16
 
 
 def dft_table(length):
-    half = length // 2
+    count = length // 4
     n = np.arange(length, dtype=np.int32)[:, None]
-    k = np.arange(half, dtype=np.int32)[None, :]
+    k = np.arange(count, dtype=np.int32)[None, :]
     phase = (n * k % length).astype(np.float32) * np.float32(2.0 * math.pi / length)
     factor = np.float32(1.0 / math.sqrt(length))
-    real = (np.cos(phase) * factor).reshape(length, half // LANES, LANES)
-    imag = (-np.sin(phase) * factor).reshape(length, half // LANES, LANES)
-    return np.concatenate([real, imag], axis=2).reshape(length, length).astype(ml_dtypes.bfloat16)
+    real = (np.cos(phase) * factor).reshape(length, count // LANES, LANES)
+    imag = (-np.sin(phase) * factor).reshape(length, count // LANES, LANES)
+    table = np.concatenate([real, imag], axis=2).reshape(length // DEPTH, DEPTH, 2 * count)
+    return table.astype(ml_dtypes.bfloat16)
 
 
 def front_kernel(
     dims, section_ref, starts_hbm, owner_hbm, taper_hbm, volts_hbm, weights_hbm, table_hbm,
-    out_ref, starts, owner, taper, volts, weights, table, rows, gain, mixed, beams, turned, sems,
+    out_ref, starts, owner, taper, volts, weights, table, gain, beams, turned, sems, *rest,
 ):
     inputs, taps, frames, length, beam_count, sections, stations = dims
     channels = length // 2
     chunks = channels // LANES
     block = channels // sections
+    depths = length // DEPTH
+    mixed, rows = rest[:chunks], rest[chunks:]
     half = 16
     parts = inputs // half
     starts_copy = pltpu.make_async_copy(starts_hbm, starts, sems.at[0])
@@ -48,19 +52,22 @@
     ]
     table_copies = [
         pltpu.make_async_copy(
-            table_hbm.at[:, pl.ds(c * 2 * LANES, 2 * LANES)], table.at[c], sems.at[4 + parts + c]
+            table_hbm.at[c], table.at[c], sems.at[4 + parts + c]
         )
-        for c in range(chunks)
+        for c in range(depths)
     ]
-    copies = [taper_copy, *volt_copies, weight_copy, *table_copies]
-    for copy in copies + [starts_copy, owner_copy]:
+    small = [taper_copy, starts_copy, owner_copy]
+    for copy in small + volt_copies + table_copies + [weight_copy]:
         copy.start()
 
-    taper_copy.wait()
-    for i in range(parts):
-        volt_copies[i].wait()
-        for c in range(length // LANES):
-            at = c * LANES
+    turns = lax.broadcasted_iota(jnp.int32, (half, LANES), 1) & 3
+    signs = [
+        jnp.where(turns == i, 1.0, jnp.where(turns == i + 2, -1.0, 0.0)).astype(BF16)
+        for i in range(2)
+    ]
+    def filter_of(d, i):
+        for c in range(DEPTH // LANES):
+            at = d * DEPTH + c * LANES
             gains = [
                 jnp.broadcast_to(taper[pl.ds(t, 1), pl.ds(at, LANES)], (half, LANES))
                 for t in range(taps)
@@ -74,9 +81,29 @@
                         term = gains[t] * value
                         sums[f] = term if sums[f] is None else sums[f] + term
             for f in range(frames):
-                rows[pl.ds(f * inputs + i * half, half), pl.ds(at, LANES)] = sums[f].astype(BF16)
-
-    starts_copy.wait()
+                plain = sums[f].astype(BF16)
+                for r, value in enumerate((plain, plain * signs[0], plain * signs[1])):
+                    place = (r * frames + f) * inputs + i * half
+                    rows[d][pl.ds(place, half), pl.ds(c * LANES, LANES)] = value
+
+    for copy in small:
+        copy.wait()
+    for i in range(parts):
+        volt_copies[i].wait()
+        filter_of(0, i)
+    spectra = None
+    for d in range(depths):
+        table_copies[d].wait()
+        if d == depths - 1:
+            weight_copy.wait()
+        term = jnp.dot(rows[d][...], table[d], preferred_element_type=F32)
+        spectra = term if spectra is None else spectra + term
+        if d + 1 < depths:
+            for i in range(parts):
+                filter_of(d + 1, i)
+    for b in range(beam_count):
+        gain[b] = weights[b].astype(F32).reshape(2 * inputs, channels)
+
     section = section_ref[0]
     keep = [
         jnp.where(((section - starts[b] + sections) & (sections - 1)) < sections // 2, 1.0, 0.0)
@@ -87,27 +114,30 @@
     even = (row & 1) == 0
     tiles = 2 * inputs // 8
 
+    def keep_spectra(c, f, real, imag):
+        for part, one, two in ((0, real, -imag), (1, imag, real)):
+            mixed[c][part, f, pl.ds(0, inputs, stride=2), :] = one
+            mixed[c][part, f, pl.ds(1, inputs, stride=2), :] = two
+
     def spectra_of(c):
-        table_copies[c].wait()
-        spectra = jnp.dot(rows[...], table[c], preferred_element_type=F32)
+        def take(r, f, part):
+            at = (r * frames + f) * inputs
+            lane = (2 * c + part) * LANES
+            return lax.slice(spectra, (at, lane), (at + inputs, lane + LANES))
+
         for f in range(frames):
-            real = lax.slice(spectra, (f * inputs, 0), ((f + 1) * inputs, LANES))
-            imag = lax.slice(spectra, (f * inputs, LANES), ((f + 1) * inputs, 2 * LANES))
-            for at, one, two in ((0, real, -imag), (1, imag, real)):
-                mixed[c % 2, at, f, pl.ds(0, inputs, stride=2), :] = one
-                mixed[c % 2, at, f, pl.ds(1, inputs, stride=2), :] = two
-
-    weight_copy.wait()
-    for b in range(beam_count):
-        gain[b] = weights[b].astype(F32).reshape(2 * inputs, channels)
-    owner_copy.wait()
-    spectra_of(0)
+            keep_spectra(c, f, take(0, f, 0), take(0, f, 1))
+            keep_spectra(
+                c + chunks // 2, f,
+                take(1, f, 0) + take(2, f, 1), take(1, f, 1) - take(2, f, 0),
+            )
+
+    for c in range(chunks // 2):
+        spectra_of(c)
     per = LANES // block
     lane = lax.broadcasted_iota(jnp.int32, (1, LANES), 1)
     slot = lax.broadcasted_iota(jnp.int32, (LANES, LANES), 0)
-    for c in range(chunks):
-        if c + 1 < chunks:
-            spectra_of(c + 1)
+    for c in sorted(range(chunks), key=lambda c: c % (chunks // 2)):
         for b in range(beam_count):
             gains = [gain[b, pl.ds(8 * i, 8), pl.ds(c * LANES, LANES)] for i in range(tiles)]
             for part in range(2):
@@ -115,7 +145,7 @@
                 for f in range(frames):
                     total = None
                     for i in range(tiles):
-                        term = gains[i] * mixed[c % 2, part, f, pl.ds(8 * i, 8), :]
+                        term = gains[i] * mixed[c][part, f, pl.ds(8 * i, 8), :]
                         total = term if total is None else total + term
                     v.append(total)
                 pairs = []
@@ -154,9 +184,8 @@
 
 def selectors(beam_count, frames, stations):
     count = beam_count * frames * 2
-    group = count // 4
     pick = np.zeros((2, 2, count, LANES), np.float32)
-    columns = np.zeros((4, 2, LANES, group), np.float32)
+    columns = np.zeros((2, LANES, count), np.float32)
     for b in range(beam_count):
         for f in range(frames):
             for part in range(2):
@@ -165,7 +194,7 @@
                     j = place_of(b, f, part, pol)
                     pick[0, pol, at, j] = 1
                     pick[1, pol, at, place_of(b, f, 1 - part, pol)] = 1 if part else -1
-                    columns[at // group, pol, j, at % group] = 1
+                    columns[pol, j, at] = 1
     spread = np.zeros((2, stations, 2 * stations), np.float32)
     for st in range(stations):
         for pol in range(2):
@@ -179,7 +208,6 @@
 def back_kernel(dims, parts_ref, pick_ref, columns_ref, spread_ref, rows_ref, out_hbm, out, sems):
     beam_count, frames, stations = dims
     count = beam_count * frames * 2
-    group = count // 4
     total = parts_ref[0].astype(F32)
     for i in range(1, parts_ref.shape[0]):
         total = total + parts_ref[i].astype(F32)
@@ -196,27 +224,33 @@
                 preferred_element_type=F32,
             )
             right = term if right is None else right + term
-    pair = lax.broadcasted_iota(jnp.int32, (group, LANES), 0) // 2
+    left = None
+    for pol in range(2):
+        chosen = jnp.dot(z, columns_ref[pol], preferred_element_type=F32).astype(BF16)
+        term = jnp.dot(spread_ref[pol], chosen, preferred_element_type=F32)
+        left = term if left is None else left + term
+    upper = lax.broadcasted_iota(jnp.int32, (count, LANES), 0) < count // 2
+    held = jnp.concatenate(
+        [jnp.where(upper, right, 0.0), jnp.where(upper, 0.0, right)], axis=1
+    ).astype(BF16)
+    pair = (lax.broadcasted_iota(jnp.int32, left.shape, 1) & (count // 2 - 1)) // 2
     ends = []
-    for g in range(4):
-        left = None
-        for pol in range(2):
-            chosen = jnp.dot(z, columns_ref[g, pol], preferred_element_type=F32).astype(BF16)
-            term = jnp.dot(spread_ref[pol], chosen, preferred_element_type=F32)
-            left = term if left is None else left + term
-        left = left.astype(BF16)
-        mine = lax.slice(right, (g * group, 0), ((g + 1) * group, LANES))
-        spaced = jnp.concatenate(
-            [jnp.where(pair == i, mine, 0.0).astype(BF16) for i in range(group // 2)], axis=1
+    for b in range(beam_count // 2):
+        streamed = jnp.concatenate(
+            [jnp.where(pair == b * frames + f, left, 0.0).astype(BF16) for f in range(frames)],
+            axis=0,
         )
-        product = jnp.dot(left, spaced, preferred_element_type=F32).astype(BF16)
-        for i in range(group // 2):
-            b, f = divmod(g * (group // 2) + i, frames)
-            out[b, f] = lax.slice(product, (0, i * LANES), (2 * stations, (i + 1) * LANES))
-            if f == frames - 1:
-                copy = pltpu.make_async_copy(out.at[b], out_hbm.at[b], sems.at[b])
-                copy.start()
-                ends.append(copy)
+        product = jnp.dot(streamed, held, preferred_element_type=F32).astype(BF16)
+        for side in range(2):
+            at = b + side * (beam_count // 2)
+            for f in range(frames):
+                out[at, f] = lax.slice(
+                    product, (f * 2 * stations, side * LANES),
+                    ((f + 1) * 2 * stations, (side + 1) * LANES),
+                )
+            copy = pltpu.make_async_copy(out.at[at], out_hbm.at[at], sems.at[at])
+            copy.start()
+            ends.append(copy)
     for copy in ends:
         copy.wait()
 
@@ -244,13 +278,13 @@
             pltpu.VMEM(taper.shape, F32),
             pltpu.VMEM((inputs, voltages.shape[2]), BF16),
             pltpu.VMEM(beam_weight_table.shape[1:], BF16),
-            pltpu.VMEM((chunks, length, 2 * LANES), BF16),
-            pltpu.VMEM((frames * inputs, length), BF16),
+            pltpu.VMEM((length // DEPTH, DEPTH, channels), BF16),
             pltpu.VMEM((beam_weight_table.shape[1], 2 * inputs, channels), F32),
-            pltpu.VMEM((2, 2, frames, 2 * inputs, LANES), F32),
             pltpu.VMEM((chunks, LANES, LANES), F32),
             pltpu.VMEM((channels, LANES), F32),
-            pltpu.SemaphoreType.DMA((4 + inputs // 16 + chunks,)),
+            pltpu.SemaphoreType.DMA((4 + inputs // 16 + length // DEPTH,)),
+            *[pltpu.VMEM((2, frames, 2 * inputs, LANES), F32)] * chunks,
+            *[pltpu.VMEM((3 * frames * inputs, DEPTH), BF16)] * (length // DEPTH),
         ],
         compiler_params=pltpu.CompilerParams(vmem_limit_bytes=16 << 20),
         name="front",

time: 50.1 us -> 49.1 us (0.980)
  Pallas kernels: 6 us -> 4.96 us
    pallas_call x1, Pallas kernels: 2.18 us -> 1.48 us  [back(): pl.pallas_call(functools.partial(back_kernel, (beam_count, frames, statio...]
where the time goes in v4:
time: 49.1 us; the launch traced here: 48.9 us
  blocking collectives  43.9 us (89%)
  Pallas kernels  4.96 us (10%)
    all_to_all x1, blocking collectives, local(): lax.all_to_all(turn(parts), 'section', split_axis=0, concat_axis=0, tiled...  28.9 us
    all_to_all x1, blocking collectives, local(): lax.all_to_all(parts, 'station', split_axis=0, concat_axis=0, tiled=True)  15 us
    pallas_call x1, Pallas kernels, front(): pl.pallas_call(functools.partial(front_kernel, dims), out_shape=jax.Shape...  3.39 us
    pallas_call x1, Pallas kernels, back(): pl.pallas_call(functools.partial(back_kernel, (beam_count, frames, statio...  1.48 us

profile of v4, /device:TPU:32, one launch (start us, length us, event | category | flops | bytes accessed | tf_op | source)
XLA Modules:
  0.0 48.9 jit_solution(3556854949282395267)
XLA Ops:
  0.0 0.0 copy-start
  0.0 0.0 copy-start.1
  0.0 0.0 copy-start.2
  0.0 0.0 copy-start.3
  0.0 3.4 %front.1 = bf16[32,16,128]{2,1,0:T(8,128)(2,1)S(1)} custom-call(s32[1]{0:T(128)} %bitcast.section_ref, s32[8]{0:T(128)} %starts_hbm.1, s32[1,512]{1,0:T(1,128)} %bitcast.3, f32[14,1024]{1,0:T(8,128)} %taper_hbm.1, bf16[1,32,17408]{2,1,0:T(8,128)(2,1)} %volts_hbm.1, bf16[1,8,32,2,512]{4,3,2,1,0:T(2,128)(2,1)} %weights_hbm.1, ...), custom_call_target="tpu_custom_call" | custom-call | tf_op jit(solution)/shard_map/front/pallas_call | solution.py:270
  3.4 15.0 %all_to_all.10.in_ref = bf16[32,16,128]{2,1,0:T(8,128)(2,1)S(1)} all-to-all(bf16[32,16,128]{2,1,0:T(8,128)(2,1)S(1)} %front.1), channel_id=1, replica_groups=mesh['station'=32,'section'=16] {'station'}, dimensions={0} | all-to-all | bytes 262144 | tf_op jit(solution)/shard_map/all_to_all | solution.py:338
  18.4 0.1 turn.1
  18.5 28.9 %all_to_all.11.parts_ref = bf16[16,32,128]{2,1,0:T(8,128)(2,1)S(1)} all-to-all(bf16[16,32,128]{2,1,0:T(8,128)(2,1)S(1)} %turn.1), channel_id=1, replica_groups=mesh['station'=32,'section'=16] {'section'}, dimensions={0} | all-to-all | bytes 262144 | tf_op jit(solution)/shard_map/all_to_all | solution.py:339
  47.4 0.0 copy-done
  47.4 0.0 copy-done.1
  47.4 0.0 copy-done.2
  47.4 0.0 copy-done.3
  47.4 1.5 %back.1 = bf16[8,4,64,128]{3,2,1,0:T(8,128)(2,1)} custom-call(bf16[16,32,128]{2,1,0:T(8,128)(2,1)S(1)} %all_to_all.11.parts_ref, bf16[256,128]{1,0:T(8,128)(2,1)S(1)} %copy-done.1, bf16[2,128,64]{2,1,0:T(8,128)(2,1)S(1)} %copy-done, bf16[2,64,32]{2,1,0:T(8,128)(2,1)S(1)} %copy-done.3, bf16[2,2,32,128]{3,2,1,0:T(8,128)(2,1)S(1)} %copy-done.2), custom_call_target="tpu_custom_call" | custom-call | tf_op jit(solution)/shard_map/back/pallas_call | solution.py:320
Async XLA Ops:
  0.0 47.4 %copy-start = (bf16[2,128,64]{2,1,0:T(8,128)(2,1)S(1)}, bf16[2,128,64]{2,1,0:T(8,128)(2,1)}, u32[]{:S(2)}) copy-start(bf16[2,128,64]{2,1,0:T(8,128)(2,1)} %constant.16.clone.columns_ref) | copy-start | bytes 98308
  0.0 47.4 %copy-start.1 = (bf16[256,128]{1,0:T(8,128)(2,1)S(1)}, bf16[256,128]{1,0:T(8,128)(2,1)}, u32[]{:S(2)}) copy-start(bf16[256,128]{1,0:T(8,128)(2,1)} %constant.15.clone.pick_ref) | copy-start | bytes 196612
  0.0 47.4 %copy-start.2 = (bf16[2,2,32,128]{3,2,1,0:T(8,128)(2,1)S(1)}, bf16[2,2,32,128]{3,2,1,0:T(8,128)(2,1)}, u32[]{:S(2)}) copy-start(bf16[2,2,32,128]{3,2,1,0:T(8,128)(2,1)} %constant.18.clone.rows_ref) | copy-start | bytes 98308
  0.0 47.4 %copy-start.3 = (bf16[2,64,32]{2,1,0:T(8,128)(2,1)S(1)}, bf16[2,64,32]{2,1,0:T(8,128)(2,1)}, u32[]{:S(2)}) copy-start(bf16[2,64,32]{2,1,0:T(8,128)(2,1)} %constant.17.clone.spread_ref) | copy-start | bytes 24580

commit v5 on v4

--- a/solution.py
+++ b/solution.py
@@ -12,8 +12,14 @@
 
 LANES = 128
 DEPTH = 256
+LEAD_SECTION = 10
+LEAD_STATION = 20
 F32 = jnp.float32
 BF16 = jnp.bfloat16
+
+
+def turned_order(count, lead):
+    return [(lead + i) % count for i in range(count)]
 
 
 def dft_table(length):
@@ -160,7 +166,8 @@
                 )
 
         owners = owner[pl.ds(0, 1), pl.ds(c * LANES, LANES)]
-        pick = jnp.where(slot == (lane // block) * block + owners, 1.0, 0.0).astype(BF16)
+        spot = (owners + (stations - LEAD_STATION % stations)) & (stations - 1)
+        pick = jnp.where(slot == (lane // block) * block + spot, 1.0, 0.0).astype(BF16)
         placed = lax.dot_general(
             pick, beams[c].astype(BF16), (((1,), (1,)), ((), ())), preferred_element_type=F32
         )
@@ -174,8 +181,8 @@
 def turn_kernel(in_ref, out_ref, rows):
     first, second, _ = in_ref.shape
     rows[...] = in_ref[...].astype(F32).reshape(first * second, LANES)
-    for i in range(second):
-        out_ref[i] = rows[pl.ds(i, first, stride=second), :].astype(BF16)
+    for i, section in enumerate(turned_order(second, LEAD_SECTION)):
+        out_ref[i] = rows[pl.ds(section, first, stride=second), :].astype(BF16)
 
 
 def place_of(beam, frame, part, pol):
@@ -196,9 +203,9 @@
                     pick[1, pol, at, place_of(b, f, 1 - part, pol)] = 1 if part else -1
                     columns[pol, j, at] = 1
     spread = np.zeros((2, stations, 2 * stations), np.float32)
-    for st in range(stations):
+    for i, station in enumerate(turned_order(stations, LEAD_STATION)):
         for pol in range(2):
-            spread[pol, st, 2 * st + pol] = 1
+            spread[pol, i, 2 * station + pol] = 1
     zero = np.zeros_like(spread)
     rows = np.stack([np.concatenate([spread, zero], 2), np.concatenate([zero, spread], 2)])
     arrays = (pick.reshape(4 * count, LANES), columns, np.swapaxes(spread, 1, 2), rows)
@@ -328,6 +335,13 @@
     )(parts, *matrices)
 
 
+def exchange(blocks, axis, lead):
+    groups = [turned_order(lax.axis_size(axis), lead)]
+    return lax.all_to_all(
+        blocks, axis, split_axis=0, concat_axis=0, tiled=True, axis_index_groups=groups
+    )
+
+
 def local(voltages, taper, beam_weight_table, starts, owner_map):
     sections = lax.axis_size("section")
     stations = lax.axis_size("station")
@@ -335,8 +349,8 @@
     parts = front(
         sections, stations, starts, section, owner_map, taper, voltages, beam_weight_table
     )
-    parts = lax.all_to_all(parts, "station", split_axis=0, concat_axis=0, tiled=True)
-    parts = lax.all_to_all(turn(parts), "section", split_axis=0, concat_axis=0, tiled=True)
+    parts = exchange(parts, "station", LEAD_STATION)
+    parts = exchange(turn(parts), "section", LEAD_SECTION)
     beam_count = beam_weight_table.shape[1]
     frames = voltages.shape[2] // taper.shape[1] - taper.shape[0] + 1
     visible = back(beam_count, frames, parts)

time: 49.1 us -> 42.1 us (0.86)
  the two profiles are of different devices: /device:TPU:32 before, /device:TPU:1 now
where the time goes in v5:
time: 42.1 us; the launch traced here: 41.6 us
  blocking collectives  36.6 us (87%)
  Pallas kernels  4.97 us (12%)
    all_to_all x2, blocking collectives, exchange(): lax.all_to_all(blocks, axis, split_axis=0, concat_axis=0, tiled=True, axi...  36.6 us
    pallas_call x1, Pallas kernels, front(): pl.pallas_call(functools.partial(front_kernel, dims), out_shape=jax.Shape...  3.39 us
    pallas_call x1, Pallas kernels, back(): pl.pallas_call(functools.partial(back_kernel, (beam_count, frames, statio...  1.48 us

profile of v5, /device:TPU:1, one launch (start us, length us, event | category | flops | bytes accessed | tf_op | source)
XLA Modules:
  0.0 41.6 jit_solution(3211526105576464656)
XLA Ops:
  0.0 0.0 copy-start
  0.0 0.0 copy-start.1
  0.0 0.0 copy-start.2
  0.0 0.0 copy-start.3
  0.0 3.4 %front.1 = bf16[32,16,128]{2,1,0:T(8,128)(2,1)S(1)} custom-call(s32[1]{0:T(128)} %bitcast.section_ref, s32[8]{0:T(128)} %starts_hbm.1, s32[1,512]{1,0:T(1,128)} %bitcast.3, f32[14,1024]{1,0:T(8,128)} %taper_hbm.1, bf16[1,32,17408]{2,1,0:T(8,128)(2,1)} %volts_hbm.1, bf16[1,8,32,2,512]{4,3,2,1,0:T(2,128)(2,1)} %weights_hbm.1, ...), custom_call_target="tpu_custom_call" | custom-call | tf_op jit(solution)/shard_map/front/pallas_call | solution.py:277
  3.4 16.4 %all_to_all.10.in_ref = bf16[32,16,128]{2,1,0:T(8,128)(2,1)S(1)} all-to-all(bf16[32,16,128]{2,1,0:T(8,128)(2,1)S(1)} %front.1), channel_id=1, replica_groups={{320,336,352,368,384,400,416,432,448,464,480,496,0,16,32,48,64,80,96,11..., dimensions={0} | all-to-all | bytes 262144 | tf_op jit(solution)/shard_map/all_to_all | solution.py:340
  19.8 0.1 turn.1
  19.9 20.2 %all_to_all.11.parts_ref = bf16[16,32,128]{2,1,0:T(8,128)(2,1)S(1)} all-to-all(bf16[16,32,128]{2,1,0:T(8,128)(2,1)S(1)} %turn.1), channel_id=1, replica_groups={{10,11,12,13,14,15,0,1,2,3,4,5,6,7,8,9},{26,27,28,29,30,31,16,17,18,19,..., dimensions={0} | all-to-all | bytes 262144 | tf_op jit(solution)/shard_map/all_to_all | solution.py:340
  40.1 0.0 copy-done
  40.1 0.0 copy-done.1
  40.1 0.0 copy-done.2
  40.2 0.0 copy-done.3
  40.2 1.5 %back.1 = bf16[8,4,64,128]{3,2,1,0:T(8,128)(2,1)} custom-call(bf16[16,32,128]{2,1,0:T(8,128)(2,1)S(1)} %all_to_all.11.parts_ref, bf16[256,128]{1,0:T(8,128)(2,1)S(1)} %copy-done.1, bf16[2,128,64]{2,1,0:T(8,128)(2,1)S(1)} %copy-done, bf16[2,64,32]{2,1,0:T(8,128)(2,1)S(1)} %copy-done.3, bf16[2,2,32,128]{3,2,1,0:T(8,128)(2,1)S(1)} %copy-done.2), custom_call_target="tpu_custom_call" | custom-call | tf_op jit(solution)/shard_map/back/pallas_call | solution.py:327
Async XLA Ops:
  0.0 40.1 %copy-start = (bf16[2,128,64]{2,1,0:T(8,128)(2,1)S(1)}, bf16[2,128,64]{2,1,0:T(8,128)(2,1)}, u32[]{:S(2)}) copy-start(bf16[2,128,64]{2,1,0:T(8,128)(2,1)} %constant.16.clone.columns_ref) | copy-start | bytes 98308
  0.0 40.1 %copy-start.1 = (bf16[256,128]{1,0:T(8,128)(2,1)S(1)}, bf16[256,128]{1,0:T(8,128)(2,1)}, u32[]{:S(2)}) copy-start(bf16[256,128]{1,0:T(8,128)(2,1)} %constant.15.clone.pick_ref) | copy-start | bytes 196612
  0.0 40.1 %copy-start.2 = (bf16[2,2,32,128]{3,2,1,0:T(8,128)(2,1)S(1)}, bf16[2,2,32,128]{3,2,1,0:T(8,128)(2,1)}, u32[]{:S(2)}) copy-start(bf16[2,2,32,128]{3,2,1,0:T(8,128)(2,1)} %constant.18.clone.rows_ref) | copy-start | bytes 98308
  0.0 40.1 %copy-start.3 = (bf16[2,64,32]{2,1,0:T(8,128)(2,1)S(1)}, bf16[2,64,32]{2,1,0:T(8,128)(2,1)}, u32[]{:S(2)}) copy-start(bf16[2,64,32]{2,1,0:T(8,128)(2,1)} %constant.17.clone.spread_ref) | copy-start | bytes 24580

commit v6 on v5

--- a/solution.py
+++ b/solution.py
@@ -13,7 +13,7 @@
 LANES = 128
 DEPTH = 256
 LEAD_SECTION = 10
-LEAD_STATION = 20
+LEAD_STATION = 21
 F32 = jnp.float32
 BF16 = jnp.bfloat16
 
@@ -36,7 +36,7 @@
 
 def front_kernel(
     dims, section_ref, starts_hbm, owner_hbm, taper_hbm, volts_hbm, weights_hbm, table_hbm,
-    out_ref, starts, owner, taper, volts, weights, table, gain, beams, turned, sems, *rest,
+    out_ref, starts, owner, taper, volts, weights, table, gain, beams, sems, *rest,
 ):
     inputs, taps, frames, length, beam_count, sections, stations = dims
     channels = length // 2
@@ -172,17 +172,10 @@
             pick, beams[c].astype(BF16), (((1,), (1,)), ((), ())), preferred_element_type=F32
         )
         for s in range(per):
-            turned[pl.ds(c * per + s, stations, stride=sections), :] = lax.slice(
+            listed = (c * per + s + sections - LEAD_SECTION % sections) % sections
+            out_ref[listed] = lax.slice(
                 placed, (s * block, 0), ((s + 1) * block, LANES)
-            )
-    out_ref[...] = turned[...].astype(BF16).reshape(stations, sections, LANES)
-
-
-def turn_kernel(in_ref, out_ref, rows):
-    first, second, _ = in_ref.shape
-    rows[...] = in_ref[...].astype(F32).reshape(first * second, LANES)
-    for i, section in enumerate(turned_order(second, LEAD_SECTION)):
-        out_ref[i] = rows[pl.ds(section, first, stride=second), :].astype(BF16)
+            ).astype(BF16)
 
 
 def place_of(beam, frame, part, pol):
@@ -212,13 +205,10 @@
     return [a.astype(ml_dtypes.bfloat16) for a in arrays]
 
 
-def back_kernel(dims, parts_ref, pick_ref, columns_ref, spread_ref, rows_ref, out_hbm, out, sems):
+def back_kernel(dims, z_ref, pick_ref, columns_ref, spread_ref, rows_ref, out_hbm, out, sems):
     beam_count, frames, stations = dims
     count = beam_count * frames * 2
-    total = parts_ref[0].astype(F32)
-    for i in range(1, parts_ref.shape[0]):
-        total = total + parts_ref[i].astype(F32)
-    z = total.astype(BF16)
+    z = z_ref[...].astype(BF16)
     turned = lax.dot_general(
         pick_ref[...], z, (((1,), (1,)), ((), ())), preferred_element_type=F32
     ).astype(BF16)
@@ -276,7 +266,7 @@
     dims = (inputs, taps, frames, length, beam_weight_table.shape[1], sections, stations)
     return pl.pallas_call(
         functools.partial(front_kernel, dims),
-        out_shape=jax.ShapeDtypeStruct((channels // sections, sections, LANES), BF16),
+        out_shape=jax.ShapeDtypeStruct((sections, channels // sections, LANES), BF16),
         in_specs=[SMEM_SPEC] + [HBM_SPEC] * 6,
         out_specs=VMEM_SPEC,
         scratch_shapes=[
@@ -288,7 +278,6 @@
             pltpu.VMEM((length // DEPTH, DEPTH, channels), BF16),
             pltpu.VMEM((beam_weight_table.shape[1], 2 * inputs, channels), F32),
             pltpu.VMEM((chunks, LANES, LANES), F32),
-            pltpu.VMEM((channels, LANES), F32),
             pltpu.SemaphoreType.DMA((4 + inputs // 16 + length // DEPTH,)),
             *[pltpu.VMEM((2, frames, 2 * inputs, LANES), F32)] * chunks,
             *[pltpu.VMEM((3 * frames * inputs, DEPTH), BF16)] * (length // DEPTH),
@@ -307,21 +296,8 @@
     )
 
 
-def turn(array):
-    first, second, _ = array.shape
-    return pl.pallas_call(
-        turn_kernel,
-        out_shape=jax.ShapeDtypeStruct((second, first, LANES), BF16),
-        in_specs=[VMEM_SPEC],
-        out_specs=VMEM_SPEC,
-        scratch_shapes=[pltpu.VMEM((first * second, LANES), F32)],
-        compiler_params=pltpu.CompilerParams(vmem_limit_bytes=4 << 20),
-        name="turn",
-    )(array)
-
-
-def back(beam_count, frames, parts):
-    stations = parts.shape[1]
+def back(beam_count, frames, z):
+    stations = z.shape[0]
     shape = (beam_count, frames, 2 * stations, 4 * stations)
     matrices = [jnp.asarray(m) for m in selectors(beam_count, frames, stations)]
     return pl.pallas_call(
@@ -332,7 +308,7 @@
         scratch_shapes=[pltpu.VMEM(shape, BF16), pltpu.SemaphoreType.DMA((beam_count,))],
         compiler_params=pltpu.CompilerParams(vmem_limit_bytes=16 << 20),
         name="back",
-    )(parts, *matrices)
+    )(z, *matrices)
 
 
 def exchange(blocks, axis, lead):
@@ -349,11 +325,12 @@
     parts = front(
         sections, stations, starts, section, owner_map, taper, voltages, beam_weight_table
     )
-    parts = exchange(parts, "station", LEAD_STATION)
-    parts = exchange(turn(parts), "section", LEAD_SECTION)
+    parts = exchange(parts, "section", LEAD_SECTION)
+    total = jnp.sum(parts.astype(F32), axis=0)
+    complete = exchange(total.reshape(stations, 1, LANES), "station", LEAD_STATION)
     beam_count = beam_weight_table.shape[1]
     frames = voltages.shape[2] // taper.shape[1] - taper.shape[0] + 1
-    visible = back(beam_count, frames, parts)
+    visible = back(beam_count, frames, complete.reshape(stations, LANES))
     return visible.reshape(1, 1, 1, *visible.shape)
 
 

time: 42.1 us -> 41.8 us (level)
  no operation moved by 1% of the time
where the time goes in v6:
time: 41.8 us; the launch traced here: 41.6 us
  blocking collectives  36.7 us (88%)
  Pallas kernels  4.8 us (11%)
    all_to_all x2, blocking collectives, exchange(): lax.all_to_all(blocks, axis, split_axis=0, concat_axis=0, tiled=True, axi...  36.7 us
    pallas_call x1, Pallas kernels, front(): pl.pallas_call(functools.partial(front_kernel, dims), out_shape=jax.Shape...  3.33 us
    pallas_call x1, Pallas kernels, back(): pl.pallas_call(functools.partial(back_kernel, (beam_count, frames, statio...  1.47 us

profile of v6, /device:TPU:1, one launch (start us, length us, event | category | flops | bytes accessed | tf_op | source)
XLA Modules:
  0.0 41.6 jit_solution(6515140184991366920)
XLA Ops:
  0.0 0.0 copy-start
  0.0 0.0 copy-start.1
  0.0 0.0 copy-start.2
  0.0 0.0 copy-start.3
  0.0 3.3 %front.1 = bf16[16,32,128]{2,1,0:T(8,128)(2,1)S(1)} custom-call(s32[1]{0:T(128)} %bitcast.section_ref, s32[8]{0:T(128)} %starts_hbm.1, s32[1,512]{1,0:T(1,128)} %bitcast.7, f32[14,1024]{1,0:T(8,128)} %taper_hbm.1, bf16[1,32,17408]{2,1,0:T(8,128)(2,1)} %volts_hbm.1, bf16[1,8,32,2,512]{4,3,2,1,0:T(2,128)(2,1)} %weights_hbm.1, ...), custom_call_target="tpu_custom_call" | custom-call | tf_op jit(solution)/shard_map/front/pallas_call | solution.py:267
  3.4 24.7 %all_to_all.10 = bf16[16,32,128]{2,1,0:T(8,128)(2,1)S(1)} all-to-all(bf16[16,32,128]{2,1,0:T(8,128)(2,1)S(1)} %front.1), channel_id=1, replica_groups={{10,11,12,13,14,15,0,1,2,3,4,5,6,7,8,9},{26,27,28,29,30,31,16,17,18,19,..., dimensions={0} | all-to-all | bytes 262144 | tf_op jit(solution)/shard_map/all_to_all | solution.py:316
  28.1 12.0 %all_to_all.11 = f32[32,1,128]{2,1,0:T(1,128)S(1)} all-to-all(f32[32,1,128]{2,1,0:T(1,128)S(1)} %bitcast.6), channel_id=1, replica_groups={{336,352,368,384,400,416,432,448,464,480,496,0,16,32,48,64,80,96,112,12..., dimensions={0} | all-to-all | bytes 32768 | tf_op jit(solution)/shard_map/all_to_all | solution.py:316
  40.1 0.0 copy-done
  40.1 0.0 copy-done.1
  40.1 0.0 copy-done.2
  40.1 0.0 copy-done.3
  40.1 1.5 %back.1 = bf16[8,4,64,128]{3,2,1,0:T(8,128)(2,1)} custom-call(f32[32,128]{1,0:T(8,128)S(1)} %bitcast.5, bf16[256,128]{1,0:T(8,128)(2,1)S(1)} %copy-done.1, bf16[2,128,64]{2,1,0:T(8,128)(2,1)S(1)} %copy-done, bf16[2,64,32]{2,1,0:T(8,128)(2,1)S(1)} %copy-done.3, bf16[2,2,32,128]{3,2,1,0:T(8,128)(2,1)S(1)} %copy-done.2), custom_call_target="tpu_custom_call" | custom-call | tf_op jit(solution)/shard_map/back/pallas_call | solution.py:303
  (1 shorter events, 0.0 us)
Async XLA Ops:
  0.0 40.1 %copy-start = (bf16[2,128,64]{2,1,0:T(8,128)(2,1)S(1)}, bf16[2,128,64]{2,1,0:T(8,128)(2,1)}, u32[]{:S(2)}) copy-start(bf16[2,128,64]{2,1,0:T(8,128)(2,1)} %constant.18.clone.columns_ref) | copy-start | bytes 98308
  0.0 40.1 %copy-start.1 = (bf16[256,128]{1,0:T(8,128)(2,1)S(1)}, bf16[256,128]{1,0:T(8,128)(2,1)}, u32[]{:S(2)}) copy-start(bf16[256,128]{1,0:T(8,128)(2,1)} %constant.17.clone.pick_ref) | copy-start | bytes 196612
  0.0 40.1 %copy-start.2 = (bf16[2,2,32,128]{3,2,1,0:T(8,128)(2,1)S(1)}, bf16[2,2,32,128]{3,2,1,0:T(8,128)(2,1)}, u32[]{:S(2)}) copy-start(bf16[2,2,32,128]{3,2,1,0:T(8,128)(2,1)} %constant.20.clone.rows_ref) | copy-start | bytes 98308
  0.0 40.1 %copy-start.3 = (bf16[2,64,32]{2,1,0:T(8,128)(2,1)S(1)}, bf16[2,64,32]{2,1,0:T(8,128)(2,1)}, u32[]{:S(2)}) copy-start(bf16[2,64,32]{2,1,0:T(8,128)(2,1)} %constant.19.clone.spread_ref) | copy-start | bytes 24580
